TPU v7x, 32 devices: a whole 2x2x4 slice. The times are simulated.
32 devices in a mesh: fsdp: 4 (over y, core), ctx: 8 (over z, x).
Axes of the slice: x: 2, y: 2, z: 4, core: 2. Of those that a mesh axis runs over, the one named last changes fastest.
Arguments:
- inputs: bfloat16 [4, 2048, 768], P('fsdp', 'ctx'), may hold values from -6 to 6
- cotangent: bfloat16 [4, 2048, 768], P('fsdp', 'ctx'), may hold values from -6 to 6
- norm1_gain: bfloat16 [768], P('fsdp'), may hold values from 0.25 to 1.75
- qkv_weight: bfloat16 [768, 2304], P('fsdp'), may hold values from -0.21875 to 0.21875
- out_weight: bfloat16 [768, 768], P('fsdp'), may hold values from -6 to 6
- norm2_gain: bfloat16 [768], P('fsdp'), may hold values from 0.25 to 1.75
- gate_up_weight: bfloat16 [768, 2304], P('fsdp'), may hold values from -0.21875 to 0.21875
- down_weight: bfloat16 [1152, 768], P(None, 'fsdp'), may hold values from -0.1875 to 0.1875
Outputs:
- output: bfloat16 [4, 2048, 768], P('fsdp', 'ctx')
- input_grad: float32 [4, 2048, 768], P('fsdp', 'ctx')
- norm1_gain_grad: float32 [768], P('fsdp')
- norm2_gain_grad: float32 [768], P('fsdp')
- qkv_weight_grad: float32 [768, 2304], P('fsdp')
- out_weight_grad: float32 [768, 768], P('fsdp')
- gate_up_weight_grad: float32 [768, 2304], P('fsdp')
- down_weight_grad: float32 [1152, 768], P(None, 'fsdp')
All inputs are finite; a program needn't handle non-finite values.
Results may differ from a plain program's by a relative error of at most 0.017.
Values may be sent and summed in bfloat16 or wider, within the bound.
A program may use at most 384 MiB of HBM per device.

v0:
```python
import math

import jax
import jax.numpy as jnp
from jax import lax
from jax.sharding import PartitionSpec as P

D = 768
HEADS = 12
HEAD_DIM = 64
FF = 1152


def layer_norm(values, norm_gain):
    center = values - jnp.mean(values, axis=-1, keepdims=True)
    spread = jnp.mean(center * center, axis=-1, keepdims=True)
    return center * lax.rsqrt(spread + 1e-05) * norm_gain


def rotate(values, cosine_table, sine_table):
    half_size = values.shape[-1] // 2
    leading = values[..., :half_size]
    trailing = values[..., half_size:]
    return jnp.concatenate(
        [
            leading * cosine_table - trailing * sine_table,
            trailing * cosine_table + leading * sine_table,
        ],
        axis=-1,
    )


def rope_tables(positions):
    indices = jnp.arange(HEAD_DIM // 2).astype(jnp.float32)
    frequency = jnp.exp(indices * (-2.0 * math.log(160000.0) / HEAD_DIM))
    angles = positions[:, None] * frequency[None, :]
    return (jnp.cos(angles)[:, None, :], jnp.sin(angles)[:, None, :])


def gelu_exact(values):
    return 0.5 * values * (1.0 + jax.scipy.special.erf(values * 0.7071067811865476))


def geglu(gate_up):
    return gelu_exact(gate_up[:, :FF]) * gate_up[:, FF:]


def split_rope(projected, cosine_table, sine_table):
    heads_view = projected.reshape(projected.shape[0], 3, HEADS, HEAD_DIM)
    return (
        rotate(heads_view[:, 0], cosine_table, sine_table) * 0.125,
        rotate(heads_view[:, 1], cosine_table, sine_table),
        heads_view[:, 2],
    )


def heads_of(flat_rows):
    return flat_rows.reshape(flat_rows.shape[0], HEADS, HEAD_DIM)


def rounded(values):
    return lax.optimization_barrier(values.astype(jnp.bfloat16)).astype(jnp.float32)


def by_blocks(pieces, carry, visit):
    row_count = pieces[0].shape[0]
    block_size = math.gcd(row_count, 2048)
    stacked = tuple(
        (
            piece_rows.reshape((row_count // block_size, block_size) + piece_rows.shape[1:])
            for piece_rows in pieces
        )
    )

    def step_block(running, record):
        number, block_parts = record
        return (visit(running, block_parts, number * block_size), None)

    running, _ = lax.scan(
        step_block, carry, (jnp.arange(row_count // block_size, dtype=jnp.int32), stacked)
    )
    return running


def score_parts(query_block, key_block, value_block, grad_block, log_block, delta_block):
    scores = jnp.einsum("qhe,khe->hqk", query_block, key_block, preferred_element_type=jnp.float32)
    probabilities = jnp.exp(scores - log_block[:, :, None])
    grad_probs = jnp.einsum(
        "qhe,khe->hqk", grad_block, value_block, preferred_element_type=jnp.float32
    )
    grad_scores = (probabilities * (grad_probs - delta_block[:, :, None])).astype(jnp.bfloat16)
    return (probabilities.astype(jnp.bfloat16), grad_scores)


def on_device(
    inputs, cotangent, norm1_gain, qkv_weight, out_weight, norm2_gain, gate_up_weight, down_weight
):
    w_qkv, w_out, w_gate_up, w_down, gain_one, gain_two = (
        lax.all_gather(qkv_weight, "fsdp", axis=0, tiled=True),
        lax.all_gather(out_weight, "fsdp", axis=0, tiled=True),
        lax.all_gather(gate_up_weight, "fsdp", axis=0, tiled=True),
        lax.all_gather(down_weight, "fsdp", axis=1, tiled=True),
        lax.all_gather(norm1_gain, "fsdp", axis=0, tiled=True),
        lax.all_gather(norm2_gain, "fsdp", axis=0, tiled=True),
    )
    local_rows = inputs.shape[1]
    first_row = lax.axis_index("ctx") * local_rows
    positions = (first_row + jnp.arange(local_rows, dtype=jnp.int32)).astype(jnp.float32)
    cosine_table, sine_table = rope_tables(positions)
    tokens = inputs[0].astype(jnp.float32)
    normed, norm_back = jax.vjp(layer_norm, tokens, gain_one.astype(jnp.float32))
    normed_low = normed.astype(jnp.bfloat16)
    projected = jnp.dot(normed_low, w_qkv, preferred_element_type=jnp.float32)
    rotated, rope_back = jax.vjp(
        lambda values: split_rope(values, cosine_table, sine_table), projected
    )
    queries = rotated[0].astype(jnp.bfloat16)
    key_heads = rotated[1].astype(jnp.bfloat16)
    value_heads = rotated[2].astype(jnp.bfloat16)
    key_rows = key_heads.reshape(local_rows, D)
    value_rows = value_heads.reshape(local_rows, D)
    stats_start = (
        jnp.full((HEADS, local_rows), -1e30, jnp.float32),
        jnp.zeros((HEADS, local_rows), jnp.float32),
    )

    def visit(running, block_parts, offset):
        peak_old, total_old = running
        scores = jnp.einsum(
            "qhe,khe->hqk", queries, heads_of(block_parts[0]), preferred_element_type=jnp.float32
        )
        peak_new = jnp.maximum(peak_old, jnp.max(scores, axis=-1))
        total_new = total_old * jnp.exp(peak_old - peak_new) + jnp.sum(
            jnp.exp(scores - peak_new[:, :, None]), axis=-1
        )
        return (peak_new, total_new)

    peak, total = by_blocks(
        (lax.all_gather(key_rows, "ctx", axis=0, tiled=True),), stats_start, visit
    )
    log_total = peak + jnp.log(total)
    head_zeros = jnp.zeros((local_rows, HEADS, HEAD_DIM), jnp.float32)

    def visit(running, block_parts, offset):
        scores = jnp.einsum(
            "qhe,khe->hqk", queries, heads_of(block_parts[0]), preferred_element_type=jnp.float32
        )
        probs_low = jnp.exp(scores - log_total[:, :, None]).astype(jnp.bfloat16)
        return running + jnp.einsum(
            "hqk,khe->qhe", probs_low, heads_of(block_parts[1]), preferred_element_type=jnp.float32
        )

    attended = by_blocks(
        (
            lax.all_gather(key_rows, "ctx", axis=0, tiled=True),
            lax.all_gather(value_rows, "ctx", axis=0, tiled=True),
        ),
        head_zeros,
        visit,
    )
    attended_low = attended.reshape(local_rows, D).astype(jnp.bfloat16)
    middle = tokens + jnp.dot(attended_low, w_out, preferred_element_type=jnp.float32)
    normed_two, norm_back_two = jax.vjp(layer_norm, middle, gain_two.astype(jnp.float32))
    normed_two_low = normed_two.astype(jnp.bfloat16)
    gate_up = jnp.dot(normed_two_low, w_gate_up, preferred_element_type=jnp.float32)
    hidden, geglu_back = jax.vjp(geglu, gate_up)
    hidden_low = hidden.astype(jnp.bfloat16)
    output = (middle + jnp.dot(hidden_low, w_down, preferred_element_type=jnp.float32)).astype(
        jnp.bfloat16
    )
    upstream = cotangent[0]
    grad_down = jnp.einsum("lf,ld->fd", hidden_low, upstream, preferred_element_type=jnp.float32)
    grad_hidden = jnp.einsum("ld,fd->lf", upstream, w_down, preferred_element_type=jnp.float32)
    grad_gate_up = geglu_back(grad_hidden)[0].astype(jnp.bfloat16)
    grad_w_gate_up = jnp.einsum(
        "ld,lf->df", normed_two_low, grad_gate_up, preferred_element_type=jnp.float32
    )
    grad_normed_two = jnp.einsum(
        "lf,df->ld", grad_gate_up, w_gate_up, preferred_element_type=jnp.float32
    )
    grad_middle_part, grad_gain_two = norm_back_two(grad_normed_two)
    grad_middle = upstream.astype(jnp.float32) + grad_middle_part
    grad_branch = grad_middle.astype(jnp.bfloat16)
    grad_w_out = jnp.einsum(
        "ld,le->de", attended_low, grad_branch, preferred_element_type=jnp.float32
    )
    grad_attended = jnp.einsum(
        "le,de->ld", grad_branch, w_out, preferred_element_type=jnp.float32
    ).astype(jnp.bfloat16)
    grad_heads = heads_of(grad_attended)
    delta_rows = jnp.sum(grad_heads.astype(jnp.float32) * attended, axis=-1).T
    span = lax.axis_size("ctx") * local_rows
    back_start = (head_zeros, jnp.zeros((span, 2, D), jnp.float32))

    def visit(running, block_parts, offset):
        grad_query, grad_kv = running
        key_block = heads_of(block_parts[0])
        value_block = heads_of(block_parts[1])
        probs_low, grad_scores = score_parts(
            queries, key_block, value_block, grad_heads, log_total, delta_rows
        )
        grad_query = grad_query + jnp.einsum(
            "hqk,khe->qhe", grad_scores, key_block, preferred_element_type=jnp.float32
        )
        grad_key = jnp.einsum(
            "hqk,qhe->khe", grad_scores, queries, preferred_element_type=jnp.float32
        )
        grad_value = jnp.einsum(
            "hqk,qhe->khe", probs_low, grad_heads, preferred_element_type=jnp.float32
        )
        update = jnp.stack([grad_key.reshape(-1, D), grad_value.reshape(-1, D)], axis=1)
        grad_kv = lax.dynamic_update_slice(grad_kv, update, (offset, 0, 0))
        return (grad_query, grad_kv)

    grad_query, grad_kv_all = by_blocks(
        (
            lax.all_gather(key_rows, "ctx", axis=0, tiled=True),
            lax.all_gather(value_rows, "ctx", axis=0, tiled=True),
        ),
        back_start,
        visit,
    )
    grad_kv = lax.psum_scatter(grad_kv_all, "ctx", scatter_dimension=0, tiled=True)
    grad_key_sum = heads_of(grad_kv[:, 0])
    grad_value_sum = heads_of(grad_kv[:, 1])
    grad_rotated = (rounded(grad_query), rounded(grad_key_sum), rounded(grad_value_sum))
    grad_projected = rope_back(grad_rotated)[0].astype(jnp.bfloat16)
    grad_w_qkv = jnp.einsum(
        "ld,lf->df", normed_low, grad_projected, preferred_element_type=jnp.float32
    )
    grad_normed = jnp.einsum("lf,df->ld", grad_projected, w_qkv, preferred_element_type=jnp.float32)
    grad_tokens_part, grad_gain_one = norm_back(grad_normed)
    input_grad = grad_middle + grad_tokens_part
    local_grads = (grad_w_qkv, grad_w_out, grad_w_gate_up, grad_down, grad_gain_one, grad_gain_two)
    shards = (
        lax.psum_scatter(
            local_grads[0].astype(jnp.bfloat16), "fsdp", scatter_dimension=0, tiled=True
        ).astype(jnp.float32),
        lax.psum_scatter(
            local_grads[1].astype(jnp.bfloat16), "fsdp", scatter_dimension=0, tiled=True
        ).astype(jnp.float32),
        lax.psum_scatter(
            local_grads[2].astype(jnp.bfloat16), "fsdp", scatter_dimension=0, tiled=True
        ).astype(jnp.float32),
        lax.psum_scatter(
            local_grads[3].astype(jnp.bfloat16), "fsdp", scatter_dimension=1, tiled=True
        ).astype(jnp.float32),
        lax.psum_scatter(
            local_grads[4].astype(jnp.bfloat16), "fsdp", scatter_dimension=0, tiled=True
        ).astype(jnp.float32),
        lax.psum_scatter(
            local_grads[5].astype(jnp.bfloat16), "fsdp", scatter_dimension=0, tiled=True
        ).astype(jnp.float32),
    )
    totals = lax.psum((shards[0], shards[1], shards[2], shards[3], shards[4], shards[5]), "ctx")
    return (
        output[None],
        input_grad[None],
        totals[4],
        totals[5],
        totals[0],
        totals[1],
        totals[2],
        totals[3],
    )


def solution(mesh):
    in_specs = (
        P("fsdp", "ctx", None),
        P("fsdp", "ctx", None),
        P("fsdp"),
        P("fsdp", None),
        P("fsdp", None),
        P("fsdp"),
        P("fsdp", None),
        P(None, "fsdp"),
    )
    out_specs = (
        P("fsdp", "ctx", None),
        P("fsdp", "ctx", None),
        P("fsdp"),
        P("fsdp"),
        P("fsdp", None),
        P("fsdp", None),
        P("fsdp", None),
        P(None, "fsdp"),
    )
    return jax.shard_map(
        on_device, mesh=mesh, in_specs=in_specs, out_specs=out_specs, check_vma=False
    )
```

profile of v0, /device:TPU:0, one launch (start us, length us, event | category | flops | bytes accessed | tf_op | source)
XLA Modules:
  0.0 872.5 jit_solution(10751971023694261299)
XLA Ops:
  11.7 8.4 all-reduce.15
  23.4 19.7 %all-gather.7.cloned.1.call-done = bf16[768,2304]{1,0:T(8,128)(2,1)} async-done(((bf16[192,2304]{1,0:T(8,128)(2,1)}), bf16[768,2304]{1,0:T(8,128)(2,1)}) %all-gather.7.cloned.1.call-update) | async-done | bytes 3538960 | tf_op jit(solution)/shard_map/all_gather | solution.py:99
  43.0 5.8 copy.18
  56.8 59.9 %all-gather.11.cloned.1.call-done = bf16[2048,768]{0,1:T(8,128)(2,1)} async-done(((bf16[256,768]{0,1:T(8,128)(2,1)}), bf16[2048,768]{0,1:T(8,128)(2,1)}) %all-gather.11.cloned.1.call-update) | async-done | bytes 3145744 | tf_op jit(solution)/shard_map/all_gather | solution.py:155
  116.8 12.5 %fusion.53 = (f32[12,256]{1,0:T(8,128)S(1)}, f32[12,256,2048]{2,1,0:T(8,128)}) fusion(bf16[2048,12,64]{0,2,1:T(8,128)(2,1)} %bitcast.108, f32[256,12,32]{0,2,1:T(8,128)S(1)} %get-tuple-element.94, f32[256,12,32]{0,2,1:T(8,128)S(1)} %get-tuple-element.93), kind=kOutput, calls=%fused_computation.108 | convolution fusion | flops 812184576 | bytes 29110272 | tf_op jit(solution)/shard_map/while/body/eval_jaxpr/qhe,khe->hqk/dot_general | solution.py:145
  129.3 10.5 %exponential_reduce_fusion = f32[12,256]{1,0:T(8,128)S(1)} fusion(f32[12,256,2048]{2,1,0:T(8,128)} %get-tuple-element.108, f32[12,256]{1,0:T(8,128)S(1)} %broadcast_maximum_fusion), kind=kLoop, calls=%fused_computation.2 | loop fusion | flops 12579840 | bytes 25190400 | tf_op jit(solution)/shard_map/while/body/eval_jaxpr/reduce_sum | solution.py:133
  139.8 40.5 %all-gather.9.cloned.1.call-done = bf16[2048,768]{0,1:T(8,128)(2,1)} async-done(((bf16[256,768]{0,1:T(8,128)(2,1)}), bf16[2048,768]{0,1:T(8,128)(2,1)}) %all-gather.9.cloned.1.call-update) | async-done | bytes 3145744 | tf_op jit(solution)/shard_map/all_gather | solution.py:156
  180.3 11.9 %fusion.54 = (bf16[256,12,64]{0,2,1:T(8,128)(2,1)S(1)}, f32[256,12,64]{0,2,1:T(8,128)S(1)}) fusion(bf16[2048,12,64]{0,2,1:T(8,128)(2,1)} %bitcast.112, f32[12,256,2048]{2,1,0:T(8,128)} %get-tuple-element.108, f32[12,256]{1,0:T(8,128)S(1)} %log_add_fusion), kind=kOutput, calls=%fused_computation.109 | convolution fusion | flops 818085888 | bytes 29503488 | tf_op jit(solution)/shard_map/while/body/eval_jaxpr/hqk,khe->qhe/dot_general | solution.py:149
  192.2 5.1 all-gather.13.cloned.1.call-done
  199.5 30.1 %all-gather.15.cloned.1.call-done = bf16[768,2304]{1,0:T(8,128)(2,1)} async-done(((bf16[192,2304]{1,0:T(8,128)(2,1)}), bf16[768,2304]{1,0:T(8,128)(2,1)}) %all-gather.15.cloned.1.call-update) | async-done | bytes 3538960 | tf_op jit(solution)/shard_map/all_gather | solution.py:101
  229.5 4.6 fusion.49
  234.1 17.6 %all-gather.17.cloned.1.call-done = bf16[1152,768]{0,1:T(8,128)(2,1)} async-done(((bf16[1152,192]{0,1:T(8,128)(2,1)}), bf16[1152,768]{0,1:T(8,128)(2,1)}) %all-gather.17.cloned.1.call-update) | async-done | bytes 1769488 | tf_op jit(solution)/shard_map/all_gather | solution.py:102
  262.8 13.1 %fusion.1 = f32[12,64,2048]{2,1,0:T(8,128)} fusion(bf16[256,12,64]{0,2,1:T(8,128)(2,1)S(1)} %bitcast.114, f32[12,256,2048]{2,1,0:T(8,128)} %get-tuple-element.108, f32[12,256]{1,0:T(8,128)S(1)} %log_add_fusion), kind=kOutput, calls=%fused_computation.8 | convolution fusion | flops 817889280 | bytes 31862784 | tf_op jit(solution)/shard_map/while/body/eval_jaxpr/hqk,qhe->khe/dot_general | solution.py:208
  276.6 15.1 %multiply_convert_fusion = bf16[12,256,2048]{2,1,0:T(8,128)(2,1)} fusion(f32[12,256,2048]{2,1,0:T(8,128)} %get-tuple-element.108, f32[12,256]{1,0:T(8,128)} %bitcast.126, f32[12,256]{1,0:T(8,128)S(1)} %log_add_fusion, bf16[256,12,64]{0,2,1:T(8,128)(2,1)S(1)} %bitcast.116, bf16[2048,12,64]{0,2,1:T(8,128)(2,1)} %bitcast.113), kind=kOutput, calls=%fused_computation | convolution fusion | flops 830472192 | bytes 41312256 | tf_op jit(solution)/shard_map/while/body/eval_jaxpr/qhe,khe->hqk/dot_general | solution.py:88
  291.7 9.5 %fusion.34 = f32[12,64,2048]{2,1,0:T(8,128)} fusion(bf16[12,256,2048]{2,1,0:T(8,128)(2,1)} %multiply_convert_fusion, f32[256,12,32]{0,2,1:T(8,128)S(1)} %copy-done.5, f32[256,12,32]{0,2,1:T(8,128)S(1)} %copy-done.3), kind=kOutput, calls=%fused_computation.80 | convolution fusion | flops 805896192 | bytes 19660800 | tf_op jit(solution)/shard_map/while/body/eval_jaxpr/hqk,qhe->khe/dot_general | solution.py:205
  301.2 11.3 %pad_maximum_fusion = f32[2048,2,768]{0,2,1:T(8,128)} fusion(f32[2048,1,768]{0,2,1:T(8,128)} %bitcast.110, f32[2048,1,768]{0,2,1:T(8,128)} %bitcast.107), kind=kLoop, calls=%fused_computation.4 | loop fusion | flops 3145728 | bytes 25165824 | tf_op jit(solution)/shard_map/while/body/eval_jaxpr/stack | solution.py:211
  322.9 9.5 %fusion.10 = bf16[256,12,64]{0,2,1:T(8,128)(2,1)S(1)} fusion(bf16[2048,12,64]{0,2,1:T(8,128)(2,1)} %bitcast.109, bf16[12,256,2048]{2,1,0:T(8,128)(2,1)} %multiply_convert_fusion), kind=kOutput, calls=%fused_computation.20 | convolution fusion | flops 805502976 | bytes 16121856 | tf_op jit(solution)/shard_map/while/body/eval_jaxpr/hqk,khe->qhe/dot_general | solution.py:202
  332.4 188.1 %reduce-scatter.6.cloned.1.call-done = f32[256,2,768]{0,2,1:T(8,128)} async-done(((f32[2048,2,768]{0,2,1:T(8,128)}), f32[256,2,768]{0,2,1:T(8,128)}) %reduce-scatter.6.cloned.1.call-update) | async-done | bytes 1572880 | tf_op jit(solution)/shard_map/reduce_scatter | solution.py:223
  530.2 18.1 %reduce-scatter.10.cloned.1.call-done = bf16[192,768]{1,0:T(8,128)(2,1)} async-done(((bf16[768,768]{1,0:T(8,128)(2,1)}), bf16[192,768]{1,0:T(8,128)(2,1)}) %reduce-scatter.10.cloned.1.call-update) | async-done | bytes 294928 | tf_op jit(solution)/shard_map/reduce_scatter | solution.py:239
  548.4 32.4 %reduce-scatter.14.cloned.1.call-done = bf16[1152,192]{0,1:T(8,128)(2,1)} async-done(((bf16[1152,768]{0,1:T(8,128)(2,1)}), bf16[1152,192]{0,1:T(8,128)(2,1)}) %reduce-scatter.14.cloned.1.call-update) | async-done | bytes 442384 | tf_op jit(solution)/shard_map/reduce_scatter | solution.py:245
  580.8 42.8 %reduce-scatter.12.cloned.1.call-done = bf16[192,2304]{1,0:T(8,128)(2,1)} async-done(((bf16[768,2304]{1,0:T(8,128)(2,1)}), bf16[192,2304]{1,0:T(8,128)(2,1)}) %reduce-scatter.12.cloned.1.call-update) | async-done | bytes 884752 | tf_op jit(solution)/shard_map/reduce_scatter | solution.py:242
  628.5 6.4 all-reduce.14
  640.2 26.3 %reduce-scatter.8.cloned.1.call-done = bf16[192,2304]{1,0:T(8,128)(2,1)} async-done(((bf16[768,2304]{1,0:T(8,128)(2,1)}), bf16[192,2304]{1,0:T(8,128)(2,1)}) %reduce-scatter.8.cloned.1.call-update) | async-done | bytes 884752 | tf_op jit(solution)/shard_map/reduce_scatter | solution.py:236
  666.5 199.4 %all-reduce.17 = (f32[192]{0:T(256)}, f32[192]{0:T(256)}, f32[192,2304]{1,0:T(8,128)}, f32[192,768]{1,0:T(8,128)}, f32[192,2304]{1,0:T(8,128)}, /*index=5*/f32[1152,192]{0,1:T(8,128)}) all-reduce(f32[192]{0:T(256)} %dynamic-slice_convert_fusion.1, f32[192]{0:T(256)} %dynamic-slice_convert_fusion, ...), channel_id=1, replica_groups=mesh['fsdp'=4,'ctx'=8] {'ctx'}, use_global_device_ids=true, to_apply=%region_14.15 | all-reduce | flops 1253760 | bytes 7523328 | tf_op jit(solution)/shard_map/psum | solution.py:255
  (143 shorter events, 58.2 us)
Async XLA Ops:
  7.2 35.9 %all-gather.7.cloned.1.call-start = ((), (), s32[]{:S(2)}) async-start(), calls=%async_computation.5 | async-start | bytes 4423680 | tf_op jit(solution)/shard_map/all_gather | solution.py:99
  7.9 108.9 %all-gather.11.cloned.1.call-start = ((), (), s32[]{:S(2)}) async-start(), calls=%async_computation.7 | async-start | bytes 3538944 | tf_op jit(solution)/shard_map/all_gather | solution.py:155
  20.0 28.8 %copy-start.20 = (f32[768]{0:T(1024)}, f32[768]{0:T(1024)S(1)}, u32[]{:S(2)}) copy-start(f32[768]{0:T(1024)S(1)} %convert_element_type.154) | copy-start | bytes 9220
  21.2 27.6 %copy-start.24 = (f32[256]{0:T(256)}, f32[256]{0:T(256)S(1)}, u32[]{:S(2)}) copy-start(f32[256]{0:T(256)S(1)} %broadcast_multiply_fusion.1) | copy-start | bytes 3076
  22.5 26.3 %copy-start.32 = (f32[256]{0:T(256)}, f32[256]{0:T(256)S(1)}, u32[]{:S(2)}) copy-start(f32[256]{0:T(256)S(1)} %fusion.17) | copy-start | bytes 3076
  22.5 26.3 %copy-start.26 = (f32[256]{0:T(256)}, f32[256]{0:T(256)S(1)}, u32[]{:S(2)}) copy-start(f32[256]{0:T(256)S(1)} %fusion.38) | copy-start | bytes 3076
  53.1 76.2 %copy-start.2 = (f32[256,12,32]{0,2,1:T(8,128)}, f32[256,12,32]{0,2,1:T(8,128)S(1)}, u32[]{:S(2)}) copy-start(f32[256,12,32]{0,2,1:T(8,128)S(1)} %get-tuple-element.93) | copy-start | bytes 1179652
  53.1 76.1 %copy-start.4 = (f32[256,12,32]{0,2,1:T(8,128)}, f32[256,12,32]{0,2,1:T(8,128)S(1)}, u32[]{:S(2)}) copy-start(f32[256,12,32]{0,2,1:T(8,128)S(1)} %get-tuple-element.94) | copy-start | bytes 1179652
  54.0 126.3 %all-gather.9.cloned.1.call-start = ((), (), s32[]{:S(2)}) async-start(), calls=%async_computation.6 | async-start | bytes 3538944 | tf_op jit(solution)/shard_map/all_gather | solution.py:156
  54.8 142.5 %all-gather.13.cloned.1.call-start = ((), (), s32[]{:S(2)}) async-start(), calls=%async_computation.8 | async-start | bytes 1474560 | tf_op jit(solution)/shard_map/all_gather | solution.py:100
  55.4 174.1 %all-gather.15.cloned.1.call-start = ((), (), s32[]{:S(2)}) async-start(), calls=%async_computation.9 | async-start | bytes 4423680 | tf_op jit(solution)/shard_map/all_gather | solution.py:101
  56.0 195.7 %all-gather.17.cloned.1.call-start = ((), (), s32[]{:S(2)}) async-start(), calls=%async_computation.10 | async-start | bytes 2211840 | tf_op jit(solution)/shard_map/all_gather | solution.py:102
  56.6 464.0 %reduce-scatter.6.cloned.1.call-start = ((), (), s32[]{:S(2)}) async-start(), calls=%async_computation.11 | async-start | bytes 14155776 | tf_op jit(solution)/shard_map/reduce_scatter | solution.py:223
  56.8 199.1 %copy-start.22 = (f32[768]{0:T(1024)}, f32[768]{0:T(1024)S(1)}, u32[]{:S(2)}) copy-start(f32[768]{0:T(1024)S(1)} %convert_element_type.165) | copy-start | bytes 9220
  199.2 56.7 %copy-start.28 = (f32[256]{0:T(256)}, f32[256]{0:T(256)S(1)}, u32[]{:S(2)}) copy-start(f32[256]{0:T(256)S(1)} %broadcast_multiply_fusion) | copy-start | bytes 3076
  199.5 56.5 %copy-start.30 = (f32[256]{0:T(256)}, f32[256]{0:T(256)S(1)}, u32[]{:S(2)}) copy-start(f32[256]{0:T(256)S(1)} %fusion.39) | copy-start | bytes 3076
  199.5 52.2 %copy-start.7 = (bf16[1,256,768]{2,1,0:T(8,128)(2,1)S(1)}, bf16[1,256,768]{2,1,0:T(8,128)(2,1)}, u32[]{:S(2)}) copy-start(bf16[1,256,768]{2,1,0:T(8,128)(2,1)} %param.9) | copy-start | bytes 1179652
  276.6 15.1 %copy-start.5 = (f32[256,12,32]{0,2,1:T(8,128)S(1)}, f32[256,12,32]{0,2,1:T(8,128)}, u32[]{:S(2)}) copy-start(f32[256,12,32]{0,2,1:T(8,128)} %copy-done.4) | copy-start | bytes 1179652
  312.5 235.9 %reduce-scatter.10.cloned.1.call-start = ((), (), s32[]{:S(2)}) async-start(), calls=%async_computation.13 | async-start | bytes 1474560 | tf_op jit(solution)/shard_map/reduce_scatter | solution.py:239
  315.0 265.8 %reduce-scatter.14.cloned.1.call-start = ((), (), s32[]{:S(2)}) async-start(), calls=%async_computation.15 | async-start | bytes 2211840 | tf_op jit(solution)/shard_map/reduce_scatter | solution.py:245
  318.2 305.4 %reduce-scatter.12.cloned.1.call-start = ((), (), s32[]{:S(2)}) async-start(), calls=%async_computation.14 | async-start | bytes 4423680 | tf_op jit(solution)/shard_map/reduce_scatter | solution.py:242
  322.5 344.0 %reduce-scatter.8.cloned.1.call-start = ((), (), s32[]{:S(2)}) async-start(), calls=%async_computation.12 | async-start | bytes 4423680 | tf_op jit(solution)/shard_map/reduce_scatter | solution.py:236
  626.8 39.7 %copy-start.14 = (bf16[192,2304]{1,0:T(8,128)(2,1)S(1)}, bf16[192,2304]{1,0:T(8,128)(2,1)}, u32[]{:S(2)}) copy-start(bf16[192,2304]{1,0:T(8,128)(2,1)} %reduce-scatter.12.cloned.1.call-done) | copy-start | bytes 2654212
  626.8 39.7 %copy-start.19 = (bf16[192,768]{1,0:T(8,128)(2,1)S(1)}, bf16[192,768]{1,0:T(8,128)(2,1)}, u32[]{:S(2)}) copy-start(bf16[192,768]{1,0:T(8,128)(2,1)} %reduce-scatter.10.cloned.1.call-done) | copy-start | bytes 884740
  (21 other events, 56.1 us)
Sparse Core Ops, SparseCore 0:
  9.5 33.4 all-gather.6
  54.1 62.6 all-gather.10
  119.4 60.8 all-gather.8
  181.7 15.6 all-gather.12
  198.8 30.7 all-gather.14
  230.9 20.7 all-gather.16
  312.6 207.8 reduce-scatter.5
  523.7 24.6 reduce-scatter.9
  551.5 29.1 reduce-scatter.13
  583.2 40.3 reduce-scatter.11
  626.2 40.3 reduce-scatter.7
where the time goes:
time: 874 us; the launch traced here: 873 us
  waiting for transfers between devices  483 us (55%)
  blocking collectives  214 us (24%)
  matrix products  107 us (12%)
  other arithmetic  37.5 us (4%)
  between operations  15.6 us (2%)
  local copies, waits for them, and re-layouts  14.5 us (2%)
    psum x1, blocking collectives, on_device(): lax.psum((shards[0], shards[1], shards[2], shards[3], shards[4], shards[5...  199 us
    reduce_scatter x1, waiting for transfers between devices, on_device(): lax.psum_scatter(grad_kv_all, 'ctx', scatter_dimension=0, tiled=True)  188 us
    all_gather x1, waiting for transfers between devices, on_device(): lax.all_gather(key_rows, 'ctx', axis=0, tiled=True)  59.9 us
    reduce_scatter x1, waiting for transfers between devices, on_device(): lax.psum_scatter(local_grads[2].astype(jnp.bfloat16), 'fsdp', scatter_dim...  42.8 us
    all_gather x1, waiting for transfers between devices, on_device(): lax.all_gather(value_rows, 'ctx', axis=0, tiled=True)  40.5 us
    reduce_scatter x1, waiting for transfers between devices, on_device(): lax.psum_scatter(local_grads[3].astype(jnp.bfloat16), 'fsdp', scatter_dim...  32.4 us
    all_gather x1, waiting for transfers between devices, on_device(): lax.all_gather(gate_up_weight, 'fsdp', axis=0, tiled=True)  30.1 us
    reduce_scatter x1, waiting for transfers between devices, on_device(): lax.psum_scatter(local_grads[0].astype(jnp.bfloat16), 'fsdp', scatter_dim...  26.3 us
  transfers between devices with their start and end apart: 11, of which 11 were waited for; matrix products, arithmetic and copies ran while one was open for 10% of the time, Pallas kernels for 0%

commit v1 on v0

--- a/solution.py
+++ b/solution.py
@@ -3,6 +3,8 @@
 import jax
 import jax.numpy as jnp
 from jax import lax
+from jax.experimental import pallas as pl
+from jax.experimental.pallas import tpu as pltpu
 from jax.sharding import PartitionSpec as P
 
 D = 768
@@ -92,16 +94,293 @@
     return (probabilities.astype(jnp.bfloat16), grad_scores)
 
 
+MESH = pl.DeviceIdType.MESH
+ANY = pl.BlockSpec(memory_space=pl.ANY)
+WHOLE = pl.BlockSpec(memory_space=pltpu.VMEM)
+
+
+def ring_neighbours():
+    n = lax.axis_size("ctx")
+    index = lax.axis_index("ctx")
+    odd = index % 2
+    place = (1 - odd) * (index // 2) + odd * (n - 1 - index // 2)
+
+    def index_of(position):
+        upper = position // (n // 2)
+        return (1 - upper) * 2 * position + upper * (2 * (n - 1 - position) + 1)
+
+    return index_of((place + 1) % n), index_of((place + n - 1) % n)
+
+
+def send_to(source, target, send_sem, recv_sem, index):
+    return pltpu.make_async_remote_copy(
+        src_ref=source,
+        dst_ref=target,
+        send_sem=send_sem,
+        recv_sem=recv_sem,
+        device_id={"ctx": index},
+        device_id_type=MESH,
+    )
+
+
+def greet(neighbours):
+    barrier = pltpu.get_barrier_semaphore()
+    for index in neighbours:
+        pl.semaphore_signal(barrier, inc=1, device_id={"ctx": index}, device_id_type=MESH)
+    pl.semaphore_wait(barrier, 2)
+
+
+def gather_kernel(n, own, slots, local_sem, send_sem, recv_sem):
+    ahead, behind = ring_neighbours()
+    half = own.shape[0] // 2
+    greet((ahead, behind))
+    keep = pltpu.make_async_copy(own, slots.at[0], local_sem)
+    keep.start()
+    parts = (pl.ds(0, half), pl.ds(half, half))
+
+    def copies(step, way):
+        found = []
+        for part in (0, 1):
+            if step == n // 2 - 1 and part != way:
+                continue
+            here, there = (step, step + 1) if way == 0 else ((n - step) % n, n - step - 1)
+            source = own if step == 0 else slots.at[here]
+            found.append(
+                send_to(
+                    source.at[parts[part]],
+                    slots.at[there, parts[part]],
+                    send_sem.at[way, step, part],
+                    recv_sem.at[way, step, part],
+                    (ahead, behind)[way],
+                )
+            )
+        return found
+
+    steps = n // 2
+    made = {}
+    for step in range(steps):
+        for part in (0, 1):
+            for way in (0, 1):
+                last = step == steps - 1
+                if last and part != way:
+                    continue
+                if step > 0:
+                    made[step - 1, way][part].wait_recv()
+                if part == 0 or last:
+                    made[step, way] = copies(step, way)
+                copy = made[step, way][0 if last else part]
+                copy.start()
+    for way in (0, 1):
+        if steps > 1:
+            made[steps - 2, way][1 - way].wait_recv()
+        made[steps - 1, way][0].wait_recv()
+    for key in made:
+        for copy in made[key]:
+            copy.wait_send()
+    keep.wait()
+
+
+def ring_gather(block):
+    n = lax.axis_size("ctx")
+    rows, columns = block.shape
+    return pl.pallas_call(
+        lambda *refs: gather_kernel(n, *refs),
+        out_shape=jax.ShapeDtypeStruct((n, rows, columns), block.dtype),
+        in_specs=[WHOLE],
+        out_specs=ANY,
+        scratch_shapes=[
+            pltpu.SemaphoreType.DMA,
+            pltpu.SemaphoreType.DMA((2, n // 2, 2)),
+            pltpu.SemaphoreType.DMA((2, n // 2, 2)),
+        ],
+        cost_estimate=pl.CostEstimate(
+            flops=70_000_000_000, bytes_accessed=2 * n * block.size, transcendentals=0
+        ),
+        compiler_params=pltpu.CompilerParams(collective_id=1, has_side_effects=True),
+        name="ring_gather",
+    )(block)
+
+
+def scatter_kernel(n, terms, total, landed, staged, load_sem, send_sem, recv_sem):
+    ahead, behind = ring_neighbours()
+    half = total.shape[1] // 2
+    parts = (pl.ds(0, half), pl.ds(half, half))
+
+    def load(step, way):
+        slot = (step + 1) % n if way == 0 else (2 * n - step - 1) % n
+        return pltpu.make_async_copy(
+            terms.at[way, slot], staged.at[way, step % 2], load_sem.at[way, step % 2]
+        )
+
+    for way in (0, 1):
+        load(0, way).start()
+    for way in (0, 1):
+        load(1, way).start()
+    greet((ahead, behind))
+    made = {}
+
+    def send(step, way, part):
+        source = staged.at[way, 0] if step == 0 else landed.at[way, step - 1]
+        copy = send_to(
+            source.at[parts[part]],
+            landed.at[way, step, parts[part]],
+            send_sem.at[way, step, part],
+            recv_sem.at[way, step, part],
+            (ahead, behind)[way],
+        )
+        copy.start()
+        made[step, way, part] = copy
+
+    for way in (0, 1):
+        load(0, way).wait()
+        for part in (0, 1):
+            send(0, way, part)
+    for step in range(1, n):
+        for way in (0, 1):
+            load(step, way).wait()
+        for part in (0, 1):
+            for way in (0, 1):
+                made[step - 1, way, part].wait_recv()
+                rows = parts[part]
+                summed = landed[way, step - 1, rows].astype(jnp.float32) + staged[
+                    way, step % 2, rows
+                ].astype(jnp.float32)
+                if step == n - 1:
+                    total[way, rows] = summed.astype(total.dtype)
+                else:
+                    landed[way, step - 1, rows] = summed.astype(landed.dtype)
+                    send(step, way, part)
+        if step + 1 < n:
+            for way in (0, 1):
+                if step == 1:
+                    for part in (0, 1):
+                        made[0, way, part].wait_send()
+                if step >= 1 and step + 1 < n:
+                    load(step + 1, way).start()
+    for key in made:
+        if key[0] > 0:
+            made[key].wait_send()
+
+
+def ring_scatter(terms, kind, ident):
+    _, n, rows, columns = terms.shape
+    return pl.pallas_call(
+        lambda *refs: scatter_kernel(n, *refs),
+        out_shape=jax.ShapeDtypeStruct((2, rows, columns), kind),
+        in_specs=[ANY],
+        out_specs=WHOLE,
+        scratch_shapes=[
+            pltpu.VMEM((2, n - 1, rows, columns), terms.dtype),
+            pltpu.VMEM((2, 2, rows, columns), terms.dtype),
+            pltpu.SemaphoreType.DMA((2, 2)),
+            pltpu.SemaphoreType.DMA((2, n - 1, 2)),
+            pltpu.SemaphoreType.DMA((2, n - 1, 2)),
+        ],
+        cost_estimate=pl.CostEstimate(
+            flops=70_000_000_000, bytes_accessed=2 * terms.size, transcendentals=0
+        ),
+        compiler_params=pltpu.CompilerParams(
+            collective_id=ident, has_side_effects=True, vmem_limit_bytes=60_000_000
+        ),
+        name="ring_scatter",
+    )(terms)
+
+
+def sum_kernel(n, terms, total, landed, send_sem, recv_sem):
+    ahead, behind = ring_neighbours()
+    index = lax.axis_index("ctx")
+    odd = index % 2
+    place = (1 - odd) * (index // 2) + odd * (n - 1 - index // 2)
+    greet((ahead, behind))
+
+    def slot(way, back):
+        return (place + n - back) % n if way == 0 else (place + back) % n
+
+    made = {}
+
+    def send(source, target, step, way):
+        copy = send_to(
+            source, target, send_sem.at[way, step], recv_sem.at[way, step], (ahead, behind)[way]
+        )
+        copy.start()
+        made[step, way] = copy
+
+    for way in (0, 1):
+        send(terms.at[way, slot(way, 1)], landed.at[way, 0], 0, way)
+    for step in range(1, n):
+        for way in (0, 1):
+            made[step - 1, way].wait_recv()
+            own = slot(way, step + 1)
+            summed = (
+                landed[way, step - 1].astype(jnp.float32) + terms[way, own].astype(jnp.float32)
+            ).astype(landed.dtype)
+            if step < n - 1:
+                landed[way, step - 1] = summed
+                send(landed.at[way, step - 1], landed.at[way, step], step, way)
+            else:
+                total[way, own] = summed
+                send(total.at[way, own], total.at[way, own], n - 1, way)
+    for step in range(n, 2 * n - 2):
+        for way in (0, 1):
+            made[step - 1, way].wait_recv()
+            have = slot(way, step - n + 1)
+            send(total.at[way, have], total.at[way, have], step, way)
+    for way in (0, 1):
+        made[2 * n - 3, way].wait_recv()
+    for key in made:
+        made[key].wait_send()
+
+
+def ring_sum(flat, ident):
+    n = lax.axis_size("ctx")
+    terms = flat.reshape(2, n, flat.size // (2 * n * 128), 128)
+    rows = terms.shape[2]
+    total = pl.pallas_call(
+        lambda *refs: sum_kernel(n, *refs),
+        out_shape=jax.ShapeDtypeStruct(terms.shape, terms.dtype),
+        in_specs=[WHOLE],
+        out_specs=WHOLE,
+        scratch_shapes=[
+            pltpu.VMEM((2, n - 1, rows, 128), terms.dtype),
+            pltpu.SemaphoreType.DMA((2, 2 * n - 2)),
+            pltpu.SemaphoreType.DMA((2, 2 * n - 2)),
+        ],
+        cost_estimate=pl.CostEstimate(
+            flops=60_000_000_000, bytes_accessed=4 * terms.size, transcendentals=0
+        ),
+        compiler_params=pltpu.CompilerParams(collective_id=ident, has_side_effects=True),
+        name="ring_sum",
+    )(terms)
+    return total.reshape(flat.shape)
+
+
+def packed_terms(pieces, column):
+    n = lax.axis_size("ctx")
+    shards = lax.axis_size("fsdp")
+    rows = pieces[0].shape[0]
+    unit = 2 * n * 16 * 128
+    width = sum(piece.shape[1] for piece in pieces) + 1
+    step = 128
+    while (rows // shards) * step % unit:
+        step += 128
+    full = -(-width // step) * step
+    tail = jnp.pad(column.astype(jnp.bfloat16)[:, None], ((0, 0), (0, full - width)))
+    return jnp.concatenate([piece.astype(jnp.bfloat16) for piece in pieces] + [tail], axis=1)
+
+
 def on_device(
     inputs, cotangent, norm1_gain, qkv_weight, out_weight, norm2_gain, gate_up_weight, down_weight
 ):
-    w_qkv, w_out, w_gate_up, w_down, gain_one, gain_two = (
-        lax.all_gather(qkv_weight, "fsdp", axis=0, tiled=True),
+    gains = jnp.pad(jnp.stack([norm1_gain, norm2_gain], axis=1), ((0, 0), (0, 126)))
+    first = lax.all_gather(
+        jnp.concatenate([qkv_weight, gains], axis=1), "fsdp", axis=0, tiled=True
+    )
+    w_qkv = first[:, : 3 * D]
+    gain_one, gain_two = first[:, 3 * D], first[:, 3 * D + 1]
+    w_out, w_gate_up, w_down = (
         lax.all_gather(out_weight, "fsdp", axis=0, tiled=True),
         lax.all_gather(gate_up_weight, "fsdp", axis=0, tiled=True),
         lax.all_gather(down_weight, "fsdp", axis=1, tiled=True),
-        lax.all_gather(norm1_gain, "fsdp", axis=0, tiled=True),
-        lax.all_gather(norm2_gain, "fsdp", axis=0, tiled=True),
     )
     local_rows = inputs.shape[1]
     first_row = lax.axis_index("ctx") * local_rows
@@ -119,6 +398,9 @@
     value_heads = rotated[2].astype(jnp.bfloat16)
     key_rows = key_heads.reshape(local_rows, D)
     value_rows = value_heads.reshape(local_rows, D)
+    span = lax.axis_size("ctx") * local_rows
+    kv_slots = ring_gather(jnp.concatenate([key_rows, value_rows], axis=1)).reshape(span, 2 * D)
+    all_keys, all_values = kv_slots[:, :D], kv_slots[:, D:]
     stats_start = (
         jnp.full((HEADS, local_rows), -1e30, jnp.float32),
         jnp.zeros((HEADS, local_rows), jnp.float32),
@@ -136,7 +418,7 @@
         return (peak_new, total_new)
 
     peak, total = by_blocks(
-        (lax.all_gather(key_rows, "ctx", axis=0, tiled=True),), stats_start, visit
+        (all_keys,), stats_start, visit
     )
     log_total = peak + jnp.log(total)
     head_zeros = jnp.zeros((local_rows, HEADS, HEAD_DIM), jnp.float32)
@@ -152,8 +434,8 @@
 
     attended = by_blocks(
         (
-            lax.all_gather(key_rows, "ctx", axis=0, tiled=True),
-            lax.all_gather(value_rows, "ctx", axis=0, tiled=True),
+            all_keys,
+            all_values,
         ),
         head_zeros,
         visit,
@@ -169,7 +451,7 @@
         jnp.bfloat16
     )
     upstream = cotangent[0]
-    grad_down = jnp.einsum("lf,ld->fd", hidden_low, upstream, preferred_element_type=jnp.float32)
+    grad_down = jnp.einsum("lf,ld->df", hidden_low, upstream, preferred_element_type=jnp.float32)
     grad_hidden = jnp.einsum("ld,fd->lf", upstream, w_down, preferred_element_type=jnp.float32)
     grad_gate_up = geglu_back(grad_hidden)[0].astype(jnp.bfloat16)
     grad_w_gate_up = jnp.einsum(
@@ -189,8 +471,7 @@
     ).astype(jnp.bfloat16)
     grad_heads = heads_of(grad_attended)
     delta_rows = jnp.sum(grad_heads.astype(jnp.float32) * attended, axis=-1).T
-    span = lax.axis_size("ctx") * local_rows
-    back_start = (head_zeros, jnp.zeros((span, 2, D), jnp.float32))
+    back_start = (head_zeros, jnp.zeros((2, span, D), jnp.bfloat16))
 
     def visit(running, block_parts, offset):
         grad_query, grad_kv = running
@@ -208,22 +489,24 @@
         grad_value = jnp.einsum(
             "hqk,qhe->khe", probs_low, grad_heads, preferred_element_type=jnp.float32
         )
-        update = jnp.stack([grad_key.reshape(-1, D), grad_value.reshape(-1, D)], axis=1)
-        grad_kv = lax.dynamic_update_slice(grad_kv, update, (offset, 0, 0))
+        update = jnp.stack([grad_key.reshape(-1, D), grad_value.reshape(-1, D)], axis=0)
+        grad_kv = lax.dynamic_update_slice(grad_kv, update.astype(jnp.bfloat16), (0, offset, 0))
         return (grad_query, grad_kv)
 
     grad_query, grad_kv_all = by_blocks(
         (
-            lax.all_gather(key_rows, "ctx", axis=0, tiled=True),
-            lax.all_gather(value_rows, "ctx", axis=0, tiled=True),
+            all_keys,
+            all_values,
         ),
         back_start,
         visit,
     )
-    grad_kv = lax.psum_scatter(grad_kv_all, "ctx", scatter_dimension=0, tiled=True)
-    grad_key_sum = heads_of(grad_kv[:, 0])
-    grad_value_sum = heads_of(grad_kv[:, 1])
-    grad_rotated = (rounded(grad_query), rounded(grad_key_sum), rounded(grad_value_sum))
+    grad_kv = ring_scatter(
+        grad_kv_all.reshape(2, -1, local_rows, D), jnp.bfloat16, 2
+    ).astype(jnp.float32)
+    grad_key_sum = heads_of(grad_kv[0])
+    grad_value_sum = heads_of(grad_kv[1])
+    grad_rotated = (rounded(grad_query), grad_key_sum, grad_value_sum)
     grad_projected = rope_back(grad_rotated)[0].astype(jnp.bfloat16)
     grad_w_qkv = jnp.einsum(
         "ld,lf->df", normed_low, grad_projected, preferred_element_type=jnp.float32
@@ -231,37 +514,27 @@
     grad_normed = jnp.einsum("lf,df->ld", grad_projected, w_qkv, preferred_element_type=jnp.float32)
     grad_tokens_part, grad_gain_one = norm_back(grad_normed)
     input_grad = grad_middle + grad_tokens_part
-    local_grads = (grad_w_qkv, grad_w_out, grad_w_gate_up, grad_down, grad_gain_one, grad_gain_two)
-    shards = (
-        lax.psum_scatter(
-            local_grads[0].astype(jnp.bfloat16), "fsdp", scatter_dimension=0, tiled=True
-        ).astype(jnp.float32),
-        lax.psum_scatter(
-            local_grads[1].astype(jnp.bfloat16), "fsdp", scatter_dimension=0, tiled=True
-        ).astype(jnp.float32),
-        lax.psum_scatter(
-            local_grads[2].astype(jnp.bfloat16), "fsdp", scatter_dimension=0, tiled=True
-        ).astype(jnp.float32),
-        lax.psum_scatter(
-            local_grads[3].astype(jnp.bfloat16), "fsdp", scatter_dimension=1, tiled=True
-        ).astype(jnp.float32),
-        lax.psum_scatter(
-            local_grads[4].astype(jnp.bfloat16), "fsdp", scatter_dimension=0, tiled=True
-        ).astype(jnp.float32),
-        lax.psum_scatter(
-            local_grads[5].astype(jnp.bfloat16), "fsdp", scatter_dimension=0, tiled=True
-        ).astype(jnp.float32),
-    )
-    totals = lax.psum((shards[0], shards[1], shards[2], shards[3], shards[4], shards[5]), "ctx")
+    shard_one = lax.psum_scatter(
+        packed_terms((grad_w_gate_up, grad_down, grad_w_out), grad_gain_two),
+        "fsdp",
+        scatter_dimension=0,
+        tiled=True,
+    )
+    shard_two = lax.psum_scatter(
+        packed_terms((grad_w_qkv,), grad_gain_one), "fsdp", scatter_dimension=0, tiled=True
+    )
+    total_one = ring_sum(shard_one, 3).astype(jnp.float32)
+    total_two = ring_sum(shard_two, 4).astype(jnp.float32)
+    up_end, down_end, out_end = 2 * FF, 3 * FF, 3 * FF + D
     return (
         output[None],
         input_grad[None],
-        totals[4],
-        totals[5],
-        totals[0],
-        totals[1],
-        totals[2],
-        totals[3],
+        total_two[:, 3 * D],
+        total_one[:, out_end],
+        total_two[:, : 3 * D],
+        total_one[:, down_end:out_end],
+        total_one[:, :up_end],
+        total_one[:, up_end:down_end].T,
     )
 
 

time: 874 us -> 541 us (0.62)
  waiting for transfers between devices: 483 us -> 68.6 us
  Pallas kernels: 0 us -> 245 us
  blocking collectives: 214 us -> 0 us
  local copies, waits for them, and re-layouts: 14.5 us -> 70.3 us
  matrix products: 107 us -> 94.6 us
    reduce_scatter x5 -> x2, waiting for transfers between devices: 308 us -> 34.7 us  [the longest x1 27.7 us: on_device(): lax.psum_scatter(packed_terms((grad_w_qkv,), grad_gain_one), 'fsdp', scat...]
    pallas_call x0 -> x4, Pallas kernels: none -> 245 us  [the longest x2 116 us: ring_sum(): pl.pallas_call(lambda *refs: sum_kernel(n, *refs), out_shape=jax.ShapeDty...]
    psum x1 -> x0, blocking collectives: 199 us -> none  [on_device(): lax.psum((shards[0], shards[1], shards[2], shards[3], shards[4], shards[5...]
    all_gather x3 -> x1, waiting for transfers between devices: 120 us -> 31.9 us  [on_device(): lax.all_gather(jnp.concatenate([qkv_weight, gains], axis=1), 'fsdp', axis...]
    all_gather x1, waiting for transfers between devices: 30.1 us -> 0.01 us  [on_device(): lax.all_gather(gate_up_weight, 'fsdp', axis=0, tiled=True)]
    slice x1 -> x11, local copies, waits for them, and re-layouts: 0.05 us -> 20.5 us  [the longest x3 13.8 us: on_device(): all_keys, all_values = (kv_slots[:, :D], kv_slots[:, D:])]
    all_gather x1, waiting for transfers between devices: 17.6 us -> 0.01 us  [on_device(): lax.all_gather(down_weight, 'fsdp', axis=1, tiled=True)]
    unnamed x2 -> x0, blocking collectives: 14.8 us -> none
  transfers between devices with their start and end apart: 11 -> 6, of which waited for: 11 -> 3; matrix products, arithmetic and copies ran while one was open for 10% -> 18% of each run, Pallas kernels for 0% -> 22%
where the time goes in v1:
time: 541 us; the launch traced here: 531 us
  Pallas kernels  245 us (45%)
  matrix products  94.6 us (17%)
  local copies, waits for them, and re-layouts  70.3 us (13%)
  waiting for transfers between devices  68.6 us (13%)
  other arithmetic  37.2 us (7%)
  between operations  15.2 us (3%)
    pallas_call x2, Pallas kernels, ring_sum(): pl.pallas_call(lambda *refs: sum_kernel(n, *refs), out_shape=jax.ShapeDty...  116 us
    pallas_call x1, Pallas kernels, ring_gather(): pl.pallas_call(lambda *refs: gather_kernel(n, *refs), out_shape=jax.Shape...  66.4 us
    pallas_call x1, Pallas kernels, ring_scatter(): pl.pallas_call(lambda *refs: scatter_kernel(n, *refs), out_shape=jax.Shap...  62.8 us
    all_gather x1, waiting for transfers between devices, on_device(): lax.all_gather(jnp.concatenate([qkv_weight, gains], axis=1), 'fsdp', axis...  31.9 us
    reduce_scatter x1, waiting for transfers between devices, on_device(): lax.psum_scatter(packed_terms((grad_w_qkv,), grad_gain_one), 'fsdp', scat...  27.7 us
    dot_general x1, matrix products, score_parts(): jnp.einsum('qhe,khe->hqk', grad_block, value_block, preferred_element_typ...  15.5 us
    slice x3, local copies, waits for them, and re-layouts, on_device(): all_keys, all_values = (kv_slots[:, :D], kv_slots[:, D:])  13.8 us
    dot_general x1, matrix products, visit(): jnp.einsum('hqk,khe->qhe', probs_low, heads_of(block_parts[1]), preferred...  12.7 us
  transfers between devices with their start and end apart: 6, of which 3 were waited for; matrix products, arithmetic and copies ran while one was open for 18% of the time, Pallas kernels for 22%

profile of v1, /device:TPU:0, one launch (start us, length us, event | category | flops | bytes accessed | tf_op | source)
XLA Modules:
  0.0 531.2 jit_solution(3790472034961801216)
XLA Ops:
  13.7 31.9 %all-gather.5.cloned.1.call-done = bf16[768,2432]{1,0:T(8,128)(2,1)} async-done(((bf16[192,2432]{1,0:T(8,128)(2,1)}), bf16[768,2432]{1,0:T(8,128)(2,1)}) %all-gather.5.cloned.1.call-update) | async-done | bytes 3735568 | tf_op jit(solution)/shard_map/all_gather | solution.py:375
  45.7 4.0 slice_bitcast_fusion
  49.7 5.8 %copy.30 = bf16[2304,768]{1,0:T(8,128)(2,1)} copy(bf16[2304,768]{0,1:T(8,128)(2,1)} %slice_bitcast_fusion) | data formatting | bytes 7077888 | tf_op jit(solution)/shard_map/dot_general | solution.py:392
  63.2 66.4 %ring_gather.1 = bf16[8,256,1536]{2,1,0:T(8,128)(2,1)} custom-call(bf16[256,1536]{1,0:T(8,128)(2,1)} %pad_maximum_fusion.1.refs_0_), custom_call_target="tpu_custom_call" | custom-call | flops 70000001024 | bytes 6291456 | tf_op jit(solution)/shard_map/ring_gather/pallas_call | solution.py:186
  129.6 5.9 %fusion.58 = (bf16[2048,768]{1,0:T(8,128)(2,1)}, bf16[2048,768]{1,0:T(8,128)(2,1)}) fusion(bf16[2048,1536]{1,0:T(8,128)(2,1)} %bitcast.133), kind=kLoop, calls=%fused_computation.124 | loop fusion | bytes 12582912 | tf_op jit(solution)/shard_map/slice | solution.py:403
  138.7 11.3 %fusion.60 = (f32[12,256]{1,0:T(8,128)S(1)}, f32[12,256,2048]{2,1,0:T(8,128)}) fusion(bf16[2048,12,64]{0,2,1:T(8,128)(2,1)S(1)} %bitcast.121, f32[256,12,32]{0,2,1:T(8,128)} %get-tuple-element.88, f32[256,12,32]{0,2,1:T(8,128)} %get-tuple-element.87), kind=kOutput, calls=%fused_computation.126 | convolution fusion | flops 812184576 | bytes 29110272 | tf_op jit(solution)/shard_map/while/body/eval_jaxpr/qhe,khe->hqk/dot_general | solution.py:427
  150.0 10.5 %exponential_reduce_fusion = f32[12,256]{1,0:T(8,128)S(1)} fusion(f32[12,256,2048]{2,1,0:T(8,128)} %get-tuple-element.100, f32[12,256]{1,0:T(8,128)S(1)} %broadcast_maximum_fusion), kind=kLoop, calls=%fused_computation.2 | loop fusion | flops 12579840 | bytes 25190400 | tf_op jit(solution)/shard_map/while/body/eval_jaxpr/reduce_sum | solution.py:415
  160.5 4.8 copy.33
  165.3 12.7 %fusion.61 = (bf16[256,12,64]{0,2,1:T(8,128)(2,1)}, f32[256,12,64]{0,2,1:T(8,128)}) fusion(bf16[2048,12,64]{0,2,1:T(8,128)(2,1)} %bitcast.123, f32[12,256,2048]{2,1,0:T(8,128)} %get-tuple-element.100, f32[12,256]{1,0:T(8,128)S(1)} %log_add_fusion), kind=kOutput, calls=%fused_computation.127 | convolution fusion | flops 818085888 | bytes 29503488 | tf_op jit(solution)/shard_map/while/body/eval_jaxpr/hqk,khe->qhe/dot_general | solution.py:431
  182.3 4.9 fusion.56
  187.2 4.3 fusion.40
  200.6 15.5 %multiply_convert_fusion = bf16[12,256,2048]{2,1,0:T(8,128)(2,1)} fusion(f32[12,256,2048]{2,1,0:T(8,128)} %get-tuple-element.100, f32[12,256]{1,0:T(8,128)} %bitcast.142, f32[12,256]{1,0:T(8,128)S(1)} %log_add_fusion, bf16[256,12,64]{0,2,1:T(8,128)(2,1)} %bitcast.131, bf16[2048,12,64]{0,2,1:T(8,128)(2,1)} %bitcast.124), kind=kOutput, calls=%fused_computation | convolution fusion | flops 830472192 | bytes 41312256 | tf_op jit(solution)/shard_map/while/body/eval_jaxpr/qhe,khe->hqk/dot_general | solution.py:90
  216.1 9.3 %fusion.17 = bf16[256,12,64]{0,2,1:T(8,128)(2,1)} fusion(bf16[2048,12,64]{0,2,1:T(8,128)(2,1)S(1)} %bitcast.122, bf16[12,256,2048]{2,1,0:T(8,128)(2,1)} %multiply_convert_fusion), kind=kOutput, calls=%fused_computation.33 | convolution fusion | flops 805502976 | bytes 16121856 | tf_op jit(solution)/shard_map/while/body/eval_jaxpr/hqk,khe->qhe/dot_general | solution.py:483
  225.5 6.9 %convolution_convert_fusion.4 = bf16[12,64,2048]{2,1,0:T(8,128)(2,1)S(1)} fusion(bf16[12,256,2048]{2,1,0:T(8,128)(2,1)} %multiply_convert_fusion, f32[256,12,32]{0,2,1:T(8,128)S(1)} %copy-done.11, f32[256,12,32]{0,2,1:T(8,128)S(1)} %copy-done.10), kind=kOutput, calls=%fused_computation.15 | convolution fusion | flops 807469056 | bytes 16515072 | tf_op jit(solution)/shard_map/while/body/eval_jaxpr/hqk,qhe->khe/dot_general | solution.py:486
  232.4 12.3 %convolution_convert_fusion.3 = bf16[12,64,2048]{2,1,0:T(8,128)(2,1)S(1)} fusion(bf16[256,12,64]{0,2,1:T(8,128)(2,1)} %bitcast.132, f32[12,256,2048]{2,1,0:T(8,128)} %get-tuple-element.100, f32[12,256]{1,0:T(8,128)S(1)} %log_add_fusion), kind=kOutput, calls=%fused_computation.14 | convolution fusion | flops 819462144 | bytes 28717056 | tf_op jit(solution)/shard_map/while/body/eval_jaxpr/hqk,qhe->khe/dot_general | solution.py:489
  249.4 5.0 copy.36
  257.2 5.3 %copy.37 = bf16[1,8,256,768]{3,2,1,0:T(8,128)(2,1)} copy(bf16[1,8,256,768]{2,1,3,0:T(8,128)(2,1)} %bitcast.129) | data formatting | bytes 6291456 | tf_op jit(solution)/shard_map/while/body/eval_jaxpr/stack | solution.py:492
  262.6 5.1 pad_maximum_fusion.refs_0_
  267.7 62.8 %ring_scatter.1 = bf16[2,256,768]{2,1,0:T(8,128)(2,1)} custom-call(bf16[2,8,256,768]{3,2,1,0:T(8,128)(2,1)} %pad_maximum_fusion.refs_0_), custom_call_target="tpu_custom_call" | custom-call | flops 70000001024 | bytes 6291456 | tf_op jit(solution)/shard_map/ring_scatter/pallas_call | solution.py:267
  354.4 27.7 %reduce-scatter.3.cloned.1.call-done = bf16[192,2560]{1,0:T(8,128)(2,1)} async-done(((bf16[768,2560]{1,0:T(8,128)(2,1)}), bf16[192,2560]{1,0:T(8,128)(2,1)}) %reduce-scatter.3.cloned.1.call-update) | async-done | bytes 983056 | tf_op jit(solution)/shard_map/reduce_scatter | solution.py:523
  385.1 52.4 %ring_sum.2 = bf16[2,8,240,128]{3,2,1,0:T(8,128)(2,1)} custom-call(bf16[2,8,240,128]{3,2,1,0:T(8,128)(2,1)} %reshape.286.refs_0_), custom_call_target="tpu_custom_call" | custom-call | flops 60000002048 | bytes 1966080 | tf_op jit(solution)/shard_map/ring_sum/pallas_call | solution.py:338
  441.7 7.0 %reduce-scatter.5.cloned.1.call-done = bf16[192,4608]{1,0:T(8,128)(2,1)} async-done(((bf16[768,4608]{1,0:T(8,128)(2,1)}), bf16[192,4608]{1,0:T(8,128)(2,1)}) %reduce-scatter.5.cloned.1.call-update) | async-done | bytes 1769488 | tf_op jit(solution)/shard_map/reduce_scatter | solution.py:517
  448.7 4.6 reshape.287.refs_0_
  453.3 63.6 %ring_sum.3 = bf16[2,8,432,128]{3,2,1,0:T(8,128)(2,1)} custom-call(bf16[2,8,432,128]{3,2,1,0:T(8,128)(2,1)} %reshape.287.refs_0_), custom_call_target="tpu_custom_call" | custom-call | flops 60000002048 | bytes 3538944 | tf_op jit(solution)/shard_map/ring_sum/pallas_call | solution.py:338
  (181 shorter events, 76.1 us)
Async XLA Ops:
  7.2 5.9 %copy-start.3 = (bf16[1,256,768]{2,1,0:T(8,128)(2,1)S(1)}, bf16[1,256,768]{2,1,0:T(8,128)(2,1)}, u32[]{:S(2)}) copy-start(bf16[1,256,768]{2,1,0:T(8,128)(2,1)} %param.8) | copy-start | bytes 1179652
  7.2 38.5 %all-gather.5.cloned.1.call-start = ((), (), s32[]{:S(2)}) async-start(), calls=%async_computation.2 | async-start | bytes 4669440 | tf_op jit(solution)/shard_map/all_gather | solution.py:375
  10.9 167.1 %all-gather.7.cloned.1.call-start = ((), (), s32[]{:S(2)}) async-start(), calls=%async_computation.3 | async-start | bytes 1474560 | tf_op jit(solution)/shard_map/all_gather | solution.py:381
  11.7 170.6 %all-gather.9.cloned.1.call-start = ((), (), s32[]{:S(2)}) async-start(), calls=%async_computation.4 | async-start | bytes 4423680 | tf_op jit(solution)/shard_map/all_gather | solution.py:382
  12.4 174.7 %all-gather.11.cloned.1.call-start = ((), (), s32[]{:S(2)}) async-start(), calls=%async_computation.5 | async-start | bytes 2211840 | tf_op jit(solution)/shard_map/all_gather | solution.py:383
  13.0 369.1 %reduce-scatter.3.cloned.1.call-start = ((), (), s32[]{:S(2)}) async-start(), calls=%async_computation.6 | async-start | bytes 4915200 | tf_op jit(solution)/shard_map/reduce_scatter | solution.py:523
  13.2 44.1 %copy-start.30 = (f32[256]{0:T(256)}, f32[256]{0:T(256)S(1)}, u32[]{:S(2)}) copy-start(f32[256]{0:T(256)S(1)} %broadcast_multiply_fusion.1) | copy-start | bytes 3076
  13.5 36.2 %copy-start.41 = (f32[256]{0:T(256)}, f32[256]{0:T(256)S(1)}, u32[]{:S(2)}) copy-start(f32[256]{0:T(256)S(1)} %fusion.25) | copy-start | bytes 3076
  13.5 43.8 %copy-start.32 = (f32[256]{0:T(256)}, f32[256]{0:T(256)S(1)}, u32[]{:S(2)}) copy-start(f32[256]{0:T(256)S(1)} %fusion.45) | copy-start | bytes 3076
  13.7 47.0 %copy-start.24 = (f32[256,32]{0,1:T(8,128)}, f32[256,32]{0,1:T(8,128)S(1)}, u32[]{:S(2)}) copy-start(f32[256,32]{0,1:T(8,128)S(1)} %get-tuple-element.97) | copy-start | bytes 98308
  13.7 47.0 %copy-start.25 = (f32[256,32]{0,1:T(8,128)}, f32[256,32]{0,1:T(8,128)S(1)}, u32[]{:S(2)}) copy-start(f32[256,32]{0,1:T(8,128)S(1)} %get-tuple-element.98) | copy-start | bytes 98308
  187.1 4.4 copy-start.1
  187.1 4.4 copy-start.12
  187.1 4.4 copy-start.28
  187.1 4.4 copy-start.35
  187.2 4.4 copy-start.37
  216.1 9.4 %copy-start.10 = (f32[256,12,32]{0,2,1:T(8,128)S(1)}, f32[256,12,32]{0,2,1:T(8,128)}, u32[]{:S(2)}) copy-start(f32[256,12,32]{0,2,1:T(8,128)} %get-tuple-element.87) | copy-start | bytes 1179652
  216.1 9.4 %copy-start.11 = (f32[256,12,32]{0,2,1:T(8,128)S(1)}, f32[256,12,32]{0,2,1:T(8,128)}, u32[]{:S(2)}) copy-start(f32[256,12,32]{0,2,1:T(8,128)} %get-tuple-element.88) | copy-start | bytes 1179652
  257.2 5.3 %copy-start.4 = (bf16[1,8,256,768]{3,2,1,0:T(8,128)(2,1)S(1)}, bf16[1,8,256,768]{3,2,1,0:T(8,128)(2,1)}, u32[]{:S(2)}) copy-start(bf16[1,8,256,768]{3,2,1,0:T(8,128)(2,1)} %copy.36) | copy-start | bytes 9437188
  340.8 107.9 %reduce-scatter.5.cloned.1.call-start = ((), (), s32[]{:S(2)}) async-start(), calls=%async_computation.7 | async-start | bytes 8847360 | tf_op jit(solution)/shard_map/reduce_scatter | solution.py:517
  349.3 3.8 copy-start.6
  349.3 3.8 copy-start.18
  349.3 3.8 copy-start.40
  349.4 3.8 copy-start.46
  (31 other events, 55.6 us)
Sparse Core Ops, SparseCore 0:
  11.1 34.5 all-gather.4
  47.2 17.4 all-gather.6
  66.3 30.7 all-gather.8
  98.5 20.7 all-gather.10
  340.9 41.1 reduce-scatter.2
  384.5 64.1 reduce-scatter.4

commit v2 on v1

--- a/solution.py
+++ b/solution.py
@@ -64,36 +64,6 @@
     return lax.optimization_barrier(values.astype(jnp.bfloat16)).astype(jnp.float32)
 
 
-def by_blocks(pieces, carry, visit):
-    row_count = pieces[0].shape[0]
-    block_size = math.gcd(row_count, 2048)
-    stacked = tuple(
-        (
-            piece_rows.reshape((row_count // block_size, block_size) + piece_rows.shape[1:])
-            for piece_rows in pieces
-        )
-    )
-
-    def step_block(running, record):
-        number, block_parts = record
-        return (visit(running, block_parts, number * block_size), None)
-
-    running, _ = lax.scan(
-        step_block, carry, (jnp.arange(row_count // block_size, dtype=jnp.int32), stacked)
-    )
-    return running
-
-
-def score_parts(query_block, key_block, value_block, grad_block, log_block, delta_block):
-    scores = jnp.einsum("qhe,khe->hqk", query_block, key_block, preferred_element_type=jnp.float32)
-    probabilities = jnp.exp(scores - log_block[:, :, None])
-    grad_probs = jnp.einsum(
-        "qhe,khe->hqk", grad_block, value_block, preferred_element_type=jnp.float32
-    )
-    grad_scores = (probabilities * (grad_probs - delta_block[:, :, None])).astype(jnp.bfloat16)
-    return (probabilities.astype(jnp.bfloat16), grad_scores)
-
-
 MESH = pl.DeviceIdType.MESH
 ANY = pl.BlockSpec(memory_space=pl.ANY)
 WHOLE = pl.BlockSpec(memory_space=pltpu.VMEM)
@@ -130,78 +100,148 @@
     pl.semaphore_wait(barrier, 2)
 
 
-def gather_kernel(n, own, slots, local_sem, send_sem, recv_sem):
+def half_of(values, half):
+    lane = lax.broadcasted_iota(jnp.int32, values.shape, 1)
+    keep = lane < HEAD_DIM if half == 0 else lane >= HEAD_DIM
+    return jnp.where(keep, values, jnp.zeros_like(values))
+
+
+def times_t(left, right):
+    return lax.dot_general(
+        left, right, (((1,), (1,)), ((), ())), preferred_element_type=jnp.float32
+    )
+
+
+def times(left, right):
+    return jnp.dot(left, right, preferred_element_type=jnp.float32)
+
+
+def attend_kernel(
+    n, own, queries, slots, attended, logs, held, peak, total, gathered, local_sem, send_sem, recv_sem
+):
     ahead, behind = ring_neighbours()
     half = own.shape[0] // 2
     greet((ahead, behind))
-    keep = pltpu.make_async_copy(own, slots.at[0], local_sem)
+    keep = pltpu.make_async_copy(own, slots.at[0], local_sem.at[2])
     keep.start()
     parts = (pl.ds(0, half), pl.ds(half, half))
-
-    def copies(step, way):
-        found = []
-        for part in (0, 1):
-            if step == n // 2 - 1 and part != way:
-                continue
-            here, there = (step, step + 1) if way == 0 else ((n - step) % n, n - step - 1)
-            source = own if step == 0 else slots.at[here]
-            found.append(
-                send_to(
-                    source.at[parts[part]],
-                    slots.at[there, parts[part]],
-                    send_sem.at[way, step, part],
-                    recv_sem.at[way, step, part],
-                    (ahead, behind)[way],
-                )
-            )
-        return found
-
     steps = n // 2
     made = {}
-    for step in range(steps):
+
+    def send(step, way, part):
+        here, there = (step, step + 1) if way == 0 else ((n - step) % n, n - step - 1)
+        source = own if step == 0 else slots.at[here]
+        copy = send_to(
+            source.at[parts[part]],
+            slots.at[there, parts[part]],
+            send_sem.at[way, step, part],
+            recv_sem.at[way, step, part],
+            (ahead, behind)[way],
+        )
+        copy.start()
+        made[step, way, part] = copy
+
+    def attend(block):
+        def pair(h, carry):
+            at = pl.multiple_of((h // 3) * D + (h % 3) * 128, 128)
+            keys = block[:, pl.ds(at, 128)]
+            values_t = block[:, pl.ds(pl.multiple_of(at + D // 2, 128), 128)].T
+            rows = queries[:, pl.ds(pl.multiple_of(h * 128, 128), 128)]
+            for side in (0, 1):
+                scores = times_t(keys, half_of(rows, side))
+                old = peak[2 * h + side]
+                new = jnp.maximum(old, jnp.max(scores, axis=0, keepdims=True))
+                weights = jnp.exp(scores - new)
+                scale = jnp.exp(old - new)
+                peak[2 * h + side] = new
+                total[2 * h + side] = total[2 * h + side] * scale + jnp.sum(
+                    weights, axis=0, keepdims=True
+                )
+                lanes = pl.ds(side * HEAD_DIM, HEAD_DIM)
+                gathered[h, lanes] = gathered[h, lanes] * scale + times(
+                    values_t[side * HEAD_DIM : (side + 1) * HEAD_DIM], weights.astype(jnp.bfloat16)
+                )
+            return carry
+
+        lax.fori_loop(0, HEADS // 2, pair, 0)
+
+    for way in (0, 1):
+        for part in (0, 1):
+            if steps > 1 or part == way:
+                send(0, way, part)
+    peak[...] = jnp.full(peak.shape, -1e30, jnp.float32)
+    total[...] = jnp.zeros(total.shape, jnp.float32)
+    gathered[...] = jnp.zeros(gathered.shape, jnp.float32)
+    attend(own)
+    for step in range(1, steps):
         for part in (0, 1):
             for way in (0, 1):
-                last = step == steps - 1
-                if last and part != way:
-                    continue
-                if step > 0:
-                    made[step - 1, way][part].wait_recv()
-                if part == 0 or last:
-                    made[step, way] = copies(step, way)
-                copy = made[step, way][0 if last else part]
-                copy.start()
+                made[step - 1, way, part].wait_recv()
+                if step < steps - 1 or part == way:
+                    send(step, way, part)
+        loads = [
+            pltpu.make_async_copy(
+                slots.at[step if way == 0 else n - step], held.at[way], local_sem.at[way]
+            )
+            for way in (0, 1)
+        ]
+        for load in loads:
+            load.start()
+        for way in (0, 1):
+            loads[way].wait()
+            attend(held.at[way])
     for way in (0, 1):
-        if steps > 1:
-            made[steps - 2, way][1 - way].wait_recv()
-        made[steps - 1, way][0].wait_recv()
+        made[steps - 1, way, way].wait_recv()
+    load = pltpu.make_async_copy(slots.at[steps], held.at[0], local_sem.at[0])
+    load.start()
+    load.wait()
+    attend(held.at[0])
+    for h in range(HEADS // 2):
+        for side in (0, 1):
+            lanes = pl.ds(side * HEAD_DIM, HEAD_DIM)
+            gathered[h, lanes] = gathered[h, lanes] / total[2 * h + side]
+        attended[:, h * 128 : (h + 1) * 128] = gathered[h].T
+    logs[...] = peak[...] + jnp.log(total[...])
     for key in made:
-        for copy in made[key]:
-            copy.wait_send()
+        made[key].wait_send()
     keep.wait()
 
 
-def ring_gather(block):
+def ring_attend(block, queries):
     n = lax.axis_size("ctx")
     rows, columns = block.shape
     return pl.pallas_call(
-        lambda *refs: gather_kernel(n, *refs),
-        out_shape=jax.ShapeDtypeStruct((n, rows, columns), block.dtype),
-        in_specs=[WHOLE],
-        out_specs=ANY,
+        lambda *refs: attend_kernel(n, *refs),
+        out_shape=(
+            jax.ShapeDtypeStruct((n, rows, columns), block.dtype),
+            jax.ShapeDtypeStruct((rows, D), jnp.float32),
+            jax.ShapeDtypeStruct((HEADS, 1, rows), jnp.float32),
+        ),
+        in_specs=[WHOLE, WHOLE],
+        out_specs=(ANY, WHOLE, WHOLE),
         scratch_shapes=[
-            pltpu.SemaphoreType.DMA,
+            pltpu.VMEM((2, rows, columns), block.dtype),
+            pltpu.VMEM((HEADS, 1, rows), jnp.float32),
+            pltpu.VMEM((HEADS, 1, rows), jnp.float32),
+            pltpu.VMEM((HEADS // 2, 128, rows), jnp.float32),
+            pltpu.SemaphoreType.DMA((3,)),
             pltpu.SemaphoreType.DMA((2, n // 2, 2)),
             pltpu.SemaphoreType.DMA((2, n // 2, 2)),
         ],
         cost_estimate=pl.CostEstimate(
             flops=70_000_000_000, bytes_accessed=2 * n * block.size, transcendentals=0
         ),
-        compiler_params=pltpu.CompilerParams(collective_id=1, has_side_effects=True),
-        name="ring_gather",
-    )(block)
-
-
-def scatter_kernel(n, terms, total, landed, staged, load_sem, send_sem, recv_sem):
+        compiler_params=pltpu.CompilerParams(
+            collective_id=1, has_side_effects=True, vmem_limit_bytes=60_000_000
+        ),
+        name="ring_attend",
+    )(block, queries)
+
+
+def back_kernel(
+    n, queries, grads, logs, deltas, slots, total, grad_queries,
+    landed, first, fresh, held, load_sem, send_sem, recv_sem,
+):
     ahead, behind = ring_neighbours()
     half = total.shape[1] // 2
     parts = (pl.ds(0, half), pl.ds(half, half))
@@ -209,18 +249,45 @@
     def load(step, way):
         slot = (step + 1) % n if way == 0 else (2 * n - step - 1) % n
         return pltpu.make_async_copy(
-            terms.at[way, slot], staged.at[way, step % 2], load_sem.at[way, step % 2]
+            slots.at[slot, :, pl.ds(way * D, D)], held.at[way], load_sem.at[way]
         )
+
+    def terms(way, target):
+        def pair(r, carry):
+            h = 3 * way + r
+            at = pl.multiple_of(r * 128, 128)
+            after = pl.multiple_of(r * 128 + D // 2, 128)
+            here = pl.ds(pl.multiple_of(h * 128, 128), 128)
+            keys = held[way, :, pl.ds(at, 128)]
+            values = held[way, :, pl.ds(after, 128)]
+            keys_t = keys.T
+            grad_key, grad_value = 0.0, 0.0
+            for side in (0, 1):
+                rows = half_of(queries[:, here], side)
+                grad_rows = half_of(grads[:, here], side)
+                probs = jnp.exp(times_t(keys, rows) - logs[2 * h + side])
+                grad_probs = times_t(values, grad_rows)
+                grad_scores = (probs * (grad_probs - deltas[2 * h + side])).astype(jnp.bfloat16)
+                grad_value += times(probs.astype(jnp.bfloat16), grad_rows)
+                grad_key += times(grad_scores, rows)
+                lanes = pl.ds(side * HEAD_DIM, HEAD_DIM)
+                grad_queries[h, lanes] += times(
+                    keys_t[side * HEAD_DIM : (side + 1) * HEAD_DIM], grad_scores
+                )
+            target[way, :, pl.ds(at, 128)] = grad_key.astype(target.dtype)
+            target[way, :, pl.ds(after, 128)] = grad_value.astype(target.dtype)
+            return carry
+
+        lax.fori_loop(0, HEADS // 4, pair, 0)
 
     for way in (0, 1):
         load(0, way).start()
-    for way in (0, 1):
-        load(1, way).start()
+    grad_queries[...] = jnp.zeros(grad_queries.shape, jnp.float32)
     greet((ahead, behind))
     made = {}
 
     def send(step, way, part):
-        source = staged.at[way, 0] if step == 0 else landed.at[way, step - 1]
+        source = first.at[way] if step == 0 else landed.at[way, step - 1]
         copy = send_to(
             source.at[parts[part]],
             landed.at[way, step, parts[part]],
@@ -233,57 +300,59 @@
 
     for way in (0, 1):
         load(0, way).wait()
+        terms(way, first)
         for part in (0, 1):
             send(0, way, part)
+        load(1, way).start()
     for step in range(1, n):
         for way in (0, 1):
             load(step, way).wait()
+            terms(way, fresh)
+            if step + 1 < n:
+                load(step + 1, way).start()
         for part in (0, 1):
             for way in (0, 1):
                 made[step - 1, way, part].wait_recv()
                 rows = parts[part]
-                summed = landed[way, step - 1, rows].astype(jnp.float32) + staged[
-                    way, step % 2, rows
-                ].astype(jnp.float32)
+                summed = landed[way, step - 1, rows].astype(jnp.float32) + fresh[way, rows].astype(
+                    jnp.float32
+                )
                 if step == n - 1:
                     total[way, rows] = summed.astype(total.dtype)
                 else:
                     landed[way, step - 1, rows] = summed.astype(landed.dtype)
                     send(step, way, part)
-        if step + 1 < n:
-            for way in (0, 1):
-                if step == 1:
-                    for part in (0, 1):
-                        made[0, way, part].wait_send()
-                if step >= 1 and step + 1 < n:
-                    load(step + 1, way).start()
     for key in made:
-        if key[0] > 0:
-            made[key].wait_send()
-
-
-def ring_scatter(terms, kind, ident):
-    _, n, rows, columns = terms.shape
+        made[key].wait_send()
+
+
+def ring_back(queries, grads, logs, deltas, slots):
+    n, rows, _ = slots.shape
     return pl.pallas_call(
-        lambda *refs: scatter_kernel(n, *refs),
-        out_shape=jax.ShapeDtypeStruct((2, rows, columns), kind),
-        in_specs=[ANY],
-        out_specs=WHOLE,
+        lambda *refs: back_kernel(n, *refs),
+        out_shape=(
+            jax.ShapeDtypeStruct((2, rows, D), jnp.bfloat16),
+            jax.ShapeDtypeStruct((HEADS // 2, 128, rows), jnp.float32),
+        ),
+        in_specs=[WHOLE, WHOLE, WHOLE, WHOLE, ANY],
+        out_specs=(WHOLE, WHOLE),
         scratch_shapes=[
-            pltpu.VMEM((2, n - 1, rows, columns), terms.dtype),
-            pltpu.VMEM((2, 2, rows, columns), terms.dtype),
-            pltpu.SemaphoreType.DMA((2, 2)),
+            pltpu.VMEM((2, n - 1, rows, D), jnp.bfloat16),
+            pltpu.VMEM((2, rows, D), jnp.bfloat16),
+            pltpu.VMEM((2, rows, D), jnp.bfloat16),
+            pltpu.VMEM((2, rows, D), jnp.bfloat16),
+            pltpu.SemaphoreType.DMA((2,)),
             pltpu.SemaphoreType.DMA((2, n - 1, 2)),
             pltpu.SemaphoreType.DMA((2, n - 1, 2)),
         ],
         cost_estimate=pl.CostEstimate(
-            flops=70_000_000_000, bytes_accessed=2 * terms.size, transcendentals=0
+            flops=80_000_000_000, bytes_accessed=2 * slots.size, transcendentals=0
         ),
         compiler_params=pltpu.CompilerParams(
-            collective_id=ident, has_side_effects=True, vmem_limit_bytes=60_000_000
-        ),
-        name="ring_scatter",
-    )(terms)
+            collective_id=2, has_side_effects=True, vmem_limit_bytes=67_000_000
+        ),
+        name="ring_back",
+    )(queries, grads, logs, deltas, slots)
 
 
 def sum_kernel(n, terms, total, landed, send_sem, recv_sem):
@@ -393,54 +462,15 @@
     rotated, rope_back = jax.vjp(
         lambda values: split_rope(values, cosine_table, sine_table), projected
     )
-    queries = rotated[0].astype(jnp.bfloat16)
-    key_heads = rotated[1].astype(jnp.bfloat16)
-    value_heads = rotated[2].astype(jnp.bfloat16)
-    key_rows = key_heads.reshape(local_rows, D)
-    value_rows = value_heads.reshape(local_rows, D)
-    span = lax.axis_size("ctx") * local_rows
-    kv_slots = ring_gather(jnp.concatenate([key_rows, value_rows], axis=1)).reshape(span, 2 * D)
-    all_keys, all_values = kv_slots[:, :D], kv_slots[:, D:]
-    stats_start = (
-        jnp.full((HEADS, local_rows), -1e30, jnp.float32),
-        jnp.zeros((HEADS, local_rows), jnp.float32),
-    )
-
-    def visit(running, block_parts, offset):
-        peak_old, total_old = running
-        scores = jnp.einsum(
-            "qhe,khe->hqk", queries, heads_of(block_parts[0]), preferred_element_type=jnp.float32
-        )
-        peak_new = jnp.maximum(peak_old, jnp.max(scores, axis=-1))
-        total_new = total_old * jnp.exp(peak_old - peak_new) + jnp.sum(
-            jnp.exp(scores - peak_new[:, :, None]), axis=-1
-        )
-        return (peak_new, total_new)
-
-    peak, total = by_blocks(
-        (all_keys,), stats_start, visit
-    )
-    log_total = peak + jnp.log(total)
-    head_zeros = jnp.zeros((local_rows, HEADS, HEAD_DIM), jnp.float32)
-
-    def visit(running, block_parts, offset):
-        scores = jnp.einsum(
-            "qhe,khe->hqk", queries, heads_of(block_parts[0]), preferred_element_type=jnp.float32
-        )
-        probs_low = jnp.exp(scores - log_total[:, :, None]).astype(jnp.bfloat16)
-        return running + jnp.einsum(
-            "hqk,khe->qhe", probs_low, heads_of(block_parts[1]), preferred_element_type=jnp.float32
-        )
-
-    attended = by_blocks(
-        (
-            all_keys,
-            all_values,
-        ),
-        head_zeros,
-        visit,
-    )
-    attended_low = attended.reshape(local_rows, D).astype(jnp.bfloat16)
+    queries = rotated[0].astype(jnp.bfloat16).reshape(local_rows, D)
+    key_rows = rotated[1].astype(jnp.bfloat16).reshape(local_rows, D)
+    value_rows = rotated[2].astype(jnp.bfloat16).reshape(local_rows, D)
+    cut = D // 2
+    block = jnp.concatenate(
+        [key_rows[:, :cut], value_rows[:, :cut], key_rows[:, cut:], value_rows[:, cut:]], axis=1
+    )
+    slots, attended, log_total = ring_attend(block, queries)
+    attended_low = attended.astype(jnp.bfloat16)
     middle = tokens + jnp.dot(attended_low, w_out, preferred_element_type=jnp.float32)
     normed_two, norm_back_two = jax.vjp(layer_norm, middle, gain_two.astype(jnp.float32))
     normed_two_low = normed_two.astype(jnp.bfloat16)
@@ -469,44 +499,23 @@
     grad_attended = jnp.einsum(
         "le,de->ld", grad_branch, w_out, preferred_element_type=jnp.float32
     ).astype(jnp.bfloat16)
-    grad_heads = heads_of(grad_attended)
-    delta_rows = jnp.sum(grad_heads.astype(jnp.float32) * attended, axis=-1).T
-    back_start = (head_zeros, jnp.zeros((2, span, D), jnp.bfloat16))
-
-    def visit(running, block_parts, offset):
-        grad_query, grad_kv = running
-        key_block = heads_of(block_parts[0])
-        value_block = heads_of(block_parts[1])
-        probs_low, grad_scores = score_parts(
-            queries, key_block, value_block, grad_heads, log_total, delta_rows
-        )
-        grad_query = grad_query + jnp.einsum(
-            "hqk,khe->qhe", grad_scores, key_block, preferred_element_type=jnp.float32
-        )
-        grad_key = jnp.einsum(
-            "hqk,qhe->khe", grad_scores, queries, preferred_element_type=jnp.float32
-        )
-        grad_value = jnp.einsum(
-            "hqk,qhe->khe", probs_low, grad_heads, preferred_element_type=jnp.float32
-        )
-        update = jnp.stack([grad_key.reshape(-1, D), grad_value.reshape(-1, D)], axis=0)
-        grad_kv = lax.dynamic_update_slice(grad_kv, update.astype(jnp.bfloat16), (0, offset, 0))
-        return (grad_query, grad_kv)
-
-    grad_query, grad_kv_all = by_blocks(
-        (
-            all_keys,
-            all_values,
-        ),
-        back_start,
-        visit,
-    )
-    grad_kv = ring_scatter(
-        grad_kv_all.reshape(2, -1, local_rows, D), jnp.bfloat16, 2
-    ).astype(jnp.float32)
-    grad_key_sum = heads_of(grad_kv[0])
-    grad_value_sum = heads_of(grad_kv[1])
-    grad_rotated = (rounded(grad_query), grad_key_sum, grad_value_sum)
+    deltas = jnp.sum(
+        heads_of(grad_attended.astype(jnp.float32) * attended), axis=-1
+    ).T[:, None, :]
+    packed_one = packed_terms((grad_w_gate_up, grad_down, grad_w_out), grad_gain_two)
+    packed_one, grad_attended, deltas = lax.optimization_barrier(
+        (packed_one, grad_attended, deltas)
+    )
+    shard_one = lax.psum_scatter(packed_one, "fsdp", scatter_dimension=0, tiled=True)
+    grad_kv, grad_query_t = ring_back(queries, grad_attended, log_total, deltas, slots)
+    grad_query = grad_query_t.reshape(D, local_rows).T
+    grad_key = jnp.concatenate([grad_kv[0, :, :cut], grad_kv[1, :, :cut]], axis=1)
+    grad_value = jnp.concatenate([grad_kv[0, :, cut:], grad_kv[1, :, cut:]], axis=1)
+    grad_rotated = (
+        rounded(heads_of(grad_query)),
+        heads_of(grad_key.astype(jnp.float32)),
+        heads_of(grad_value.astype(jnp.float32)),
+    )
     grad_projected = rope_back(grad_rotated)[0].astype(jnp.bfloat16)
     grad_w_qkv = jnp.einsum(
         "ld,lf->df", normed_low, grad_projected, preferred_element_type=jnp.float32
@@ -514,12 +523,6 @@
     grad_normed = jnp.einsum("lf,df->ld", grad_projected, w_qkv, preferred_element_type=jnp.float32)
     grad_tokens_part, grad_gain_one = norm_back(grad_normed)
     input_grad = grad_middle + grad_tokens_part
-    shard_one = lax.psum_scatter(
-        packed_terms((grad_w_gate_up, grad_down, grad_w_out), grad_gain_two),
-        "fsdp",
-        scatter_dimension=0,
-        tiled=True,
-    )
     shard_two = lax.psum_scatter(
         packed_terms((grad_w_qkv,), grad_gain_one), "fsdp", scatter_dimension=0, tiled=True
     )

time: 541 us -> 444 us (0.82)
  matrix products: 94.6 us -> 26.3 us
  local copies, waits for them, and re-layouts: 70.3 us -> 40.3 us
  other arithmetic: 37.2 us -> 20.6 us
  Pallas kernels: 245 us -> 257 us
  waiting for transfers between devices: 68.6 us -> 76.7 us
    dot_general x6 -> x0, matrix products: 68.1 us -> none  [the longest x1 15.5 us: score_parts(): jnp.einsum('qhe,khe->hqk', grad_block, value_block, preferred_element_typ...]
    slice x6 -> x7, local copies, waits for them, and re-layouts: 15.7 us -> 2 us  [the longest x2 1.51 us: on_device(): grad_kv[0, :, cut:]]
    pallas_call x2, Pallas kernels: 129 us -> 141 us  [the longest x1 73 us: ring_attend(): pl.pallas_call(lambda *refs: attend_kernel(n, *refs), out_shape=(jax.Shap...]
    reduce_sum x2 -> x1, other arithmetic: 12.4 us -> 1.35 us  [on_device(): jnp.sum(heads_of(grad_attended.astype(jnp.float32) * attended), axis=-1)]
    another operation x2 -> x0, local copies, waits for them, and re-layouts: 10.4 us -> none  [visit(): jnp.stack([grad_key.reshape(-1, D), grad_value.reshape(-1, D)], axis=0)]
    reduce_scatter x1, waiting for transfers between devices: 27.7 us -> 35.5 us  [on_device(): lax.psum_scatter(packed_terms((grad_w_qkv,), grad_gain_one), 'fsdp', scat...]
    unnamed x101 -> x63, local copies, waits for them, and re-layouts: 11.4 us -> 4.23 us
  transfers between devices with their start and end apart: 6 -> 6, of which waited for: 3 -> 3; matrix products, arithmetic and copies ran while one was open for 18% -> 8% of each run, Pallas kernels for 22% -> 29%
where the time goes in v2:
time: 444 us; the launch traced here: 436 us
  Pallas kernels  257 us (58%)
  waiting for transfers between devices  76.7 us (17%)
  local copies, waits for them, and re-layouts  40.3 us (9%)
  matrix products  26.3 us (6%)
  other arithmetic  20.6 us (5%)
  between operations  15.2 us (3%)
    pallas_call x2, Pallas kernels, ring_sum(): pl.pallas_call(lambda *refs: sum_kernel(n, *refs), out_shape=jax.ShapeDty...  116 us
    pallas_call x1, Pallas kernels, ring_attend(): pl.pallas_call(lambda *refs: attend_kernel(n, *refs), out_shape=(jax.Shap...  73 us
    pallas_call x1, Pallas kernels, ring_back(): pl.pallas_call(lambda *refs: back_kernel(n, *refs), out_shape=(jax.ShapeD...  67.7 us
    reduce_scatter x1, waiting for transfers between devices, on_device(): lax.psum_scatter(packed_terms((grad_w_qkv,), grad_gain_one), 'fsdp', scat...  35.5 us
    all_gather x1, waiting for transfers between devices, on_device(): lax.all_gather(jnp.concatenate([qkv_weight, gains], axis=1), 'fsdp', axis...  31.9 us
    concatenate x2, other arithmetic, packed_terms(): jnp.concatenate([piece.astype(jnp.bfloat16) for piece in pieces] + [tail]...  10.7 us
    dot_general x2, local copies, waits for them, and re-layouts, on_device(): projected = jnp.dot(normed_low, w_qkv, preferred_element_type=jnp.float32)  9.89 us
  transfers between devices with their start and end apart: 6, of which 3 were waited for; matrix products, arithmetic and copies ran while one was open for 8% of the time, Pallas kernels for 29%

profile of v2, /device:TPU:0, one launch (start us, length us, event | category | flops | bytes accessed | tf_op | source)
XLA Modules:
  0.0 436.4 jit_solution(6817145382253653840)
XLA Ops:
  8.7 2.2 fusion.19
  13.8 31.9 %all-gather.5.cloned.1.call-done = bf16[768,2432]{1,0:T(8,128)(2,1)} async-done(((bf16[192,2432]{1,0:T(8,128)(2,1)}), bf16[768,2432]{1,0:T(8,128)(2,1)}) %all-gather.5.cloned.1.call-update) | async-done | bytes 3735568 | tf_op jit(solution)/shard_map/all_gather | solution.py:444
  45.7 4.1 slice_bitcast_fusion
  49.8 5.8 %copy.27 = bf16[2304,768]{1,0:T(8,128)(2,1)} copy(bf16[2304,768]{0,1:T(8,128)(2,1)} %slice_bitcast_fusion) | data formatting | bytes 7077888 | tf_op jit(solution)/shard_map/dot_general | solution.py:461
  57.5 3.3 fusion.29
  63.9 73.0 %ring_attend.1 = (bf16[8,256,1536]{2,1,0:T(8,128)(2,1)}, f32[256,768]{1,0:T(8,128)}, f32[12,1,256]{2,1,0:T(1,128)}) custom-call(bf16[256,1536]{1,0:T(8,128)(2,1)} %pad_maximum_fusion.refs_0_, bf16[256,768]{1,0:T(8,128)(2,1)} %copy.32.refs_1_.refs_0_), custom_call_target="tpu_custom_call" | custom-call | flops 70000001024 | bytes 6291456 | tf_op jit(solution)/shard_map/ring_attend/pallas_call | solution.py:213
  137.0 2.1 fusion.51
  139.3 3.2 fusion.46
  142.6 3.4 fusion.35
  145.9 3.1 convolution_convert_fusion.1
  151.7 1.5 convolution_convert_fusion.3
  157.6 1.9 fusion.6
  159.5 8.6 %fusion.2 = bf16[768,4608]{1,0:T(8,128)(2,1)} fusion(bf16[768,1]{1,0:T(8,128)(2,1)} %convert_element_type.234, bf16[768,768]{1,0:T(8,128)(2,1)} %convolution_convert_fusion.3, bf16[768,1152]{1,0:T(8,128)(2,1)S(1)} %fusion.6, bf16[768,2304]{1,0:T(8,128)(2,1)S(1)} %copy-done.2), kind=kLoop, calls=%fused_computation.4 | loop fusion | flops 35389440 | bytes 13567488 | tf_op jit(solution)/shard_map/concatenate | solution.py:437
  168.1 67.7 %ring_back.1 = (bf16[2,256,768]{2,1,0:T(8,128)(2,1)}, f32[6,128,256]{2,1,0:T(8,128)}) custom-call(bf16[256,768]{1,0:T(8,128)(2,1)} %copy.32.refs_1_.refs_0_, bf16[256,768]{1,0:T(8,128)(2,1)} %get-tuple-element.17.refs_1_, f32[12,1,256]{2,1,0:T(1,128)} %get-tuple-element.18.refs_2_, f32[12,1,256]{2,1,0:T(1,128)} %broadcast_in_dim.42.refs_3_, ...), custom_call_target="tpu_custom_call" | custom-call | flops 80000000000 | bytes 6291456 | tf_op jit(solution)/shard_map/ring_back/pallas_call | solution.py:331
  243.9 2.1 fusion.3
  247.4 2.9 fusion.11
  251.6 35.5 %reduce-scatter.3.cloned.1.call-done = bf16[192,2560]{1,0:T(8,128)(2,1)} async-done(((bf16[768,2560]{1,0:T(8,128)(2,1)}), bf16[192,2560]{1,0:T(8,128)(2,1)}) %reduce-scatter.3.cloned.1.call-update) | async-done | bytes 983056 | tf_op jit(solution)/shard_map/reduce_scatter | solution.py:526
  287.1 3.0 reshape.271.refs_0_
  290.1 52.4 %ring_sum.2 = bf16[2,8,240,128]{3,2,1,0:T(8,128)(2,1)} custom-call(bf16[2,8,240,128]{3,2,1,0:T(8,128)(2,1)} %reshape.271.refs_0_), custom_call_target="tpu_custom_call" | custom-call | flops 60000002048 | bytes 1966080 | tf_op jit(solution)/shard_map/ring_sum/pallas_call | solution.py:407
  342.5 2.1 reshape.275
  346.7 7.0 %reduce-scatter.5.cloned.1.call-done = bf16[192,4608]{1,0:T(8,128)(2,1)} async-done(((bf16[768,4608]{1,0:T(8,128)(2,1)}), bf16[192,4608]{1,0:T(8,128)(2,1)}) %reduce-scatter.5.cloned.1.call-update) | async-done | bytes 1769488 | tf_op jit(solution)/shard_map/reduce_scatter | solution.py:509
  353.7 4.6 %reshape.272.refs_0_ = bf16[2,8,432,128]{3,2,1,0:T(8,128)(2,1)} reshape(bf16[192,4608]{1,0:T(8,128)(2,1)} %reduce-scatter.5.cloned.1.call-done) | data formatting | bytes 3538944 | tf_op jit(solution)/shard_map/reshape | solution.py:405
  358.3 63.6 %ring_sum.3 = bf16[2,8,432,128]{3,2,1,0:T(8,128)(2,1)} custom-call(bf16[2,8,432,128]{3,2,1,0:T(8,128)(2,1)} %reshape.272.refs_0_), custom_call_target="tpu_custom_call" | custom-call | flops 60000002048 | bytes 3538944 | tf_op jit(solution)/shard_map/ring_sum/pallas_call | solution.py:407
  421.9 3.4 reshape.276
  (135 shorter events, 32.7 us)
Async XLA Ops:
  7.2 38.5 %all-gather.5.cloned.1.call-start = ((), (), s32[]{:S(2)}) async-start(), calls=%async_computation.2 | async-start | bytes 4669440 | tf_op jit(solution)/shard_map/all_gather | solution.py:444
  8.7 4.4 %copy-start.3 = (bf16[1,256,768]{2,1,0:T(8,128)(2,1)S(1)}, bf16[1,256,768]{2,1,0:T(8,128)(2,1)}, u32[]{:S(2)}) copy-start(bf16[1,256,768]{2,1,0:T(8,128)(2,1)} %param.8) | copy-start | bytes 1179652
  10.9 126.0 %all-gather.7.cloned.1.call-start = ((), (), s32[]{:S(2)}) async-start(), calls=%async_computation.3 | async-start | bytes 1474560 | tf_op jit(solution)/shard_map/all_gather | solution.py:450
  11.7 127.6 %all-gather.9.cloned.1.call-start = ((), (), s32[]{:S(2)}) async-start(), calls=%async_computation.4 | async-start | bytes 4423680 | tf_op jit(solution)/shard_map/all_gather | solution.py:451
  12.4 130.1 %all-gather.11.cloned.1.call-start = ((), (), s32[]{:S(2)}) async-start(), calls=%async_computation.5 | async-start | bytes 2211840 | tf_op jit(solution)/shard_map/all_gather | solution.py:452
  13.0 274.1 %reduce-scatter.3.cloned.1.call-start = ((), (), s32[]{:S(2)}) async-start(), calls=%async_computation.6 | async-start | bytes 4915200 | tf_op jit(solution)/shard_map/reduce_scatter | solution.py:526
  13.2 43.7 %copy-start.21 = (f32[256]{0:T(256)}, f32[256]{0:T(256)S(1)}, u32[]{:S(2)}) copy-start(f32[256]{0:T(256)S(1)} %broadcast_multiply_fusion.1) | copy-start | bytes 3076
  13.5 36.3 %copy-start.25 = (f32[256]{0:T(256)}, f32[256]{0:T(256)S(1)}, u32[]{:S(2)}) copy-start(f32[256]{0:T(256)S(1)} %fusion.20) | copy-start | bytes 3076
  13.5 43.4 %copy-start.23 = (f32[256]{0:T(256)}, f32[256]{0:T(256)S(1)}, u32[]{:S(2)}) copy-start(f32[256]{0:T(256)S(1)} %fusion.39) | copy-start | bytes 3076
  13.7 47.2 %copy-start.15 = (f32[256,32]{0,1:T(8,128)}, f32[256,32]{0,1:T(8,128)S(1)}, u32[]{:S(2)}) copy-start(f32[256,32]{0,1:T(8,128)S(1)} %get-tuple-element.57) | copy-start | bytes 98308
  13.7 47.2 %copy-start.17 = (f32[256,32]{0,1:T(8,128)}, f32[256,32]{0,1:T(8,128)S(1)}, u32[]{:S(2)}) copy-start(f32[256,32]{0,1:T(8,128)S(1)} %get-tuple-element.58) | copy-start | bytes 98308
  139.1 11.2 %copy-start = (f32[256,768]{1,0:T(8,128)}, f32[256,768]{1,0:T(8,128)S(1)}, u32[]{:S(2)}) copy-start(f32[256,768]{1,0:T(8,128)S(1)} %get-tuple-element.60) | copy-start | bytes 2359300
  139.3 3.2 copy-start.11
  145.9 3.1 copy-start.10
  150.3 1.5 copy-start.5
  150.6 2.7 copy-start.6
  151.5 1.7 copy-start.8
  155.7 3.9 copy-start.2
  235.8 2.0 copy-start.14
  240.0 2.1 copy-start.9
  246.1 107.6 %reduce-scatter.5.cloned.1.call-start = ((), (), s32[]{:S(2)}) async-start(), calls=%async_computation.7 | async-start | bytes 8847360 | tf_op jit(solution)/shard_map/reduce_scatter | solution.py:509
  246.7 3.6 copy-start.7
  246.7 3.6 copy-start.12
  246.7 3.6 copy-start.28
  (11 other events, 10.6 us)
Sparse Core Ops, SparseCore 0:
  11.1 34.5 all-gather.4
  47.2 17.4 all-gather.6
  66.3 30.8 all-gather.8
  98.6 20.6 all-gather.10
  246.2 40.8 reduce-scatter.2
  289.5 64.1 reduce-scatter.4

commit v3 on v2

--- a/solution.py
+++ b/solution.py
@@ -365,37 +365,51 @@
     def slot(way, back):
         return (place + n - back) % n if way == 0 else (place + back) % n
 
+    rows = terms.shape[2]
+    cut = 16 * (rows // 32)
+    parts = (pl.ds(0, cut), pl.ds(cut, rows - cut))
     made = {}
 
-    def send(source, target, step, way):
+    def send(source, target, step, way, part):
         copy = send_to(
-            source, target, send_sem.at[way, step], recv_sem.at[way, step], (ahead, behind)[way]
+            source,
+            target,
+            send_sem.at[way, step, part],
+            recv_sem.at[way, step, part],
+            (ahead, behind)[way],
         )
         copy.start()
-        made[step, way] = copy
-
-    for way in (0, 1):
-        send(terms.at[way, slot(way, 1)], landed.at[way, 0], 0, way)
+        made[step, way, part] = copy
+
+    both = [(part, way) for part in (0, 1) for way in (0, 1)]
+    for part, way in both:
+        piece = parts[part]
+        send(terms.at[way, slot(way, 1), piece], landed.at[way, 0, piece], 0, way, part)
     for step in range(1, n):
-        for way in (0, 1):
-            made[step - 1, way].wait_recv()
+        for part, way in both:
+            piece = parts[part]
+            made[step - 1, way, part].wait_recv()
             own = slot(way, step + 1)
             summed = (
-                landed[way, step - 1].astype(jnp.float32) + terms[way, own].astype(jnp.float32)
+                landed[way, step - 1, piece].astype(jnp.float32)
+                + terms[way, own, piece].astype(jnp.float32)
             ).astype(landed.dtype)
             if step < n - 1:
-                landed[way, step - 1] = summed
-                send(landed.at[way, step - 1], landed.at[way, step], step, way)
+                landed[way, step - 1, piece] = summed
+                send(
+                    landed.at[way, step - 1, piece], landed.at[way, step, piece], step, way, part
+                )
             else:
-                total[way, own] = summed
-                send(total.at[way, own], total.at[way, own], n - 1, way)
+                total[way, own, piece] = summed
+                send(total.at[way, own, piece], total.at[way, own, piece], n - 1, way, part)
     for step in range(n, 2 * n - 2):
-        for way in (0, 1):
-            made[step - 1, way].wait_recv()
+        for part, way in both:
+            made[step - 1, way, part].wait_recv()
             have = slot(way, step - n + 1)
-            send(total.at[way, have], total.at[way, have], step, way)
-    for way in (0, 1):
-        made[2 * n - 3, way].wait_recv()
+            piece = parts[part]
+            send(total.at[way, have, piece], total.at[way, have, piece], step, way, part)
+    for part, way in both:
+        made[2 * n - 3, way, part].wait_recv()
     for key in made:
         made[key].wait_send()
 
@@ -411,8 +425,8 @@
         out_specs=WHOLE,
         scratch_shapes=[
             pltpu.VMEM((2, n - 1, rows, 128), terms.dtype),
-            pltpu.SemaphoreType.DMA((2, 2 * n - 2)),
-            pltpu.SemaphoreType.DMA((2, 2 * n - 2)),
+            pltpu.SemaphoreType.DMA((2, 2 * n - 2, 2)),
+            pltpu.SemaphoreType.DMA((2, 2 * n - 2, 2)),
         ],
         cost_estimate=pl.CostEstimate(
             flops=60_000_000_000, bytes_accessed=4 * terms.size, transcendentals=0
@@ -508,6 +522,9 @@
     )
     shard_one = lax.psum_scatter(packed_one, "fsdp", scatter_dimension=0, tiled=True)
     grad_kv, grad_query_t = ring_back(queries, grad_attended, log_total, deltas, slots)
+    shard_one, grad_kv, grad_query_t = lax.optimization_barrier(
+        (shard_one, grad_kv, grad_query_t)
+    )
     grad_query = grad_query_t.reshape(D, local_rows).T
     grad_key = jnp.concatenate([grad_kv[0, :, :cut], grad_kv[1, :, :cut]], axis=1)
     grad_value = jnp.concatenate([grad_kv[0, :, cut:], grad_kv[1, :, cut:]], axis=1)
@@ -523,9 +540,10 @@
     grad_normed = jnp.einsum("lf,df->ld", grad_projected, w_qkv, preferred_element_type=jnp.float32)
     grad_tokens_part, grad_gain_one = norm_back(grad_normed)
     input_grad = grad_middle + grad_tokens_part
-    shard_two = lax.psum_scatter(
-        packed_terms((grad_w_qkv,), grad_gain_one), "fsdp", scatter_dimension=0, tiled=True
-    )
+    shard_one, packed_two = lax.optimization_barrier(
+        (shard_one, packed_terms((grad_w_qkv,), grad_gain_one))
+    )
+    shard_two = lax.psum_scatter(packed_two, "fsdp", scatter_dimension=0, tiled=True)
     total_one = ring_sum(shard_one, 3).astype(jnp.float32)
     total_two = ring_sum(shard_two, 4).astype(jnp.float32)
     up_end, down_end, out_end = 2 * FF, 3 * FF, 3 * FF + D

time: 444 us -> 392 us (0.88)
  waiting for transfers between devices: 76.7 us -> 34 us
  Pallas kernels: 257 us -> 242 us
  local copies, waits for them, and re-layouts: 40.3 us -> 47.2 us
    reduce_scatter x1, waiting for transfers between devices: 35.5 us -> 0.01 us  [on_device(): lax.psum_scatter(packed_two, 'fsdp', scatter_dimension=0, tiled=True)]
    pallas_call x2, Pallas kernels: 116 us -> 101 us  [ring_sum(): pl.pallas_call(lambda *refs: sum_kernel(n, *refs), out_shape=jax.ShapeDty...]
    reduce_scatter x1, waiting for transfers between devices: 6.98 us -> 0.02 us  [on_device(): lax.psum_scatter(packed_one, 'fsdp', scatter_dimension=0, tiled=True)]
  transfers between devices with their start and end apart: 6 -> 6, of which waited for: 3 -> 1; matrix products, arithmetic and copies ran while one was open for 8% -> 12% of each run, Pallas kernels for 29% -> 51%
where the time goes in v3:
time: 392 us; the launch traced here: 385 us
  Pallas kernels  242 us (62%)
  local copies, waits for them, and re-layouts  47.2 us (12%)
  waiting for transfers between devices  34 us (9%)
  matrix products  26.3 us (7%)
  other arithmetic  20.5 us (5%)
  between operations  15.2 us (4%)
    pallas_call x2, Pallas kernels, ring_sum(): pl.pallas_call(lambda *refs: sum_kernel(n, *refs), out_shape=jax.ShapeDty...  101 us
    pallas_call x1, Pallas kernels, ring_attend(): pl.pallas_call(lambda *refs: attend_kernel(n, *refs), out_shape=(jax.Shap...  73 us
    pallas_call x1, Pallas kernels, ring_back(): pl.pallas_call(lambda *refs: back_kernel(n, *refs), out_shape=(jax.ShapeD...  68 us
    all_gather x1, waiting for transfers between devices, on_device(): lax.all_gather(jnp.concatenate([qkv_weight, gains], axis=1), 'fsdp', axis...  31.9 us
    concatenate x2, other arithmetic, packed_terms(): jnp.concatenate([piece.astype(jnp.bfloat16) for piece in pieces] + [tail]...  10.6 us
    dot_general x2, local copies, waits for them, and re-layouts, on_device(): projected = jnp.dot(normed_low, w_qkv, preferred_element_type=jnp.float32)  9.89 us
  transfers between devices with their start and end apart: 6, of which 1 were waited for; matrix products, arithmetic and copies ran while one was open for 12% of the time, Pallas kernels for 51%

profile of v3, /device:TPU:0, one launch (start us, length us, event | category | flops | bytes accessed | tf_op | source)
XLA Modules:
  0.0 385.0 jit_solution(1501549552613716471)
XLA Ops:
  8.7 2.2 fusion.19
  13.8 31.9 %all-gather.5.cloned.1.call-done = bf16[768,2432]{1,0:T(8,128)(2,1)} async-done(((bf16[192,2432]{1,0:T(8,128)(2,1)}), bf16[768,2432]{1,0:T(8,128)(2,1)}) %all-gather.5.cloned.1.call-update) | async-done | bytes 3735568 | tf_op jit(solution)/shard_map/all_gather | solution.py:458
  45.7 4.1 %slice_bitcast_fusion = bf16[2304,768]{0,1:T(8,128)(2,1)} fusion(bf16[768,2432]{1,0:T(8,128)(2,1)} %all-gather.5.cloned.1.call-done), kind=kLoop, calls=%fused_computation.11 | loop fusion | bytes 7077888 | tf_op jit(solution)/shard_map/dot_general | solution.py:475
  49.8 5.8 %copy.27 = bf16[2304,768]{1,0:T(8,128)(2,1)} copy(bf16[2304,768]{0,1:T(8,128)(2,1)} %slice_bitcast_fusion) | data formatting | bytes 7077888 | tf_op jit(solution)/shard_map/dot_general | solution.py:475
  57.5 3.3 fusion.29
  63.9 73.0 %ring_attend.1 = (bf16[8,256,1536]{2,1,0:T(8,128)(2,1)}, f32[256,768]{1,0:T(8,128)}, f32[12,1,256]{2,1,0:T(1,128)}) custom-call(bf16[256,1536]{1,0:T(8,128)(2,1)} %pad_maximum_fusion.refs_0_, bf16[256,768]{1,0:T(8,128)(2,1)} %copy.32.refs_1_.refs_0_), custom_call_target="tpu_custom_call" | custom-call | flops 70000001024 | bytes 6291456 | tf_op jit(solution)/shard_map/ring_attend/pallas_call | solution.py:213
  137.0 2.1 fusion.51
  139.4 3.2 fusion.46
  142.6 3.4 fusion.35
  145.9 3.0 convolution_convert_fusion.1
  157.6 1.9 fusion.6
  159.5 8.6 %fusion.2 = bf16[768,4608]{1,0:T(8,128)(2,1)} fusion(bf16[768,1]{1,0:T(8,128)(2,1)} %convert_element_type.234, bf16[768,768]{1,0:T(8,128)(2,1)} %convolution_convert_fusion.3, bf16[768,1152]{1,0:T(8,128)(2,1)S(1)} %fusion.6, bf16[768,2304]{1,0:T(8,128)(2,1)S(1)} %copy-done.2), kind=kLoop, calls=%fused_computation.4 | loop fusion | flops 35389440 | bytes 13567488 | tf_op jit(solution)/shard_map/concatenate | solution.py:451
  168.2 68.0 %ring_back.1 = (bf16[2,256,768]{2,1,0:T(8,128)(2,1)}, f32[6,128,256]{2,1,0:T(8,128)}) custom-call(bf16[256,768]{1,0:T(8,128)(2,1)} %copy.32.refs_1_.refs_0_, bf16[256,768]{1,0:T(8,128)(2,1)} %get-tuple-element.23.refs_1_, f32[12,1,256]{2,1,0:T(1,128)} %get-tuple-element.24.refs_2_, f32[12,1,256]{2,1,0:T(1,128)} %broadcast_in_dim.42.refs_3_, ...), custom_call_target="tpu_custom_call" | custom-call | flops 80000000000 | bytes 6291456 | tf_op jit(solution)/shard_map/ring_back/pallas_call | solution.py:331
  244.2 2.0 fusion.3
  247.5 2.9 fusion.11
  250.5 4.7 %reshape.272.refs_0_ = bf16[2,8,432,128]{3,2,1,0:T(8,128)(2,1)} reshape(bf16[192,4608]{1,0:T(8,128)(2,1)} %reduce-scatter.3.cloned.1.call-done) | data formatting | bytes 3538944 | tf_op jit(solution)/shard_map/reshape | solution.py:419
  255.2 53.9 %ring_sum.3 = bf16[2,8,432,128]{3,2,1,0:T(8,128)(2,1)} custom-call(bf16[2,8,432,128]{3,2,1,0:T(8,128)(2,1)} %reshape.272.refs_0_), custom_call_target="tpu_custom_call" | custom-call | flops 60000002048 | bytes 3538944 | tf_op jit(solution)/shard_map/ring_sum/pallas_call | solution.py:421
  309.1 4.8 %reshape.276 = f32[192,4608]{1,0:T(8,128)} reshape(bf16[2,8,432,128]{3,2,1,0:T(8,128)(2,1)} %ring_sum.3) | data formatting | bytes 5308416 | tf_op jit(solution)/shard_map/convert_element_type | solution.py:547
  313.9 1.9 slice.124
  315.8 2.9 slice.125
  321.5 2.1 slice_bitcast_fusion.1
  323.7 3.0 reshape.271.refs_0_
  326.7 46.9 %ring_sum.2 = bf16[2,8,240,128]{3,2,1,0:T(8,128)(2,1)} custom-call(bf16[2,8,240,128]{3,2,1,0:T(8,128)(2,1)} %reshape.271.refs_0_), custom_call_target="tpu_custom_call" | custom-call | flops 60000002048 | bytes 1966080 | tf_op jit(solution)/shard_map/ring_sum/pallas_call | solution.py:421
  373.6 2.1 reshape.275
  (135 shorter events, 32.1 us)
Async XLA Ops:
  7.2 38.5 %all-gather.5.cloned.1.call-start = ((), (), s32[]{:S(2)}) async-start(), calls=%async_computation.2 | async-start | bytes 4669440 | tf_op jit(solution)/shard_map/all_gather | solution.py:458
  8.7 4.4 %copy-start.3 = (bf16[1,256,768]{2,1,0:T(8,128)(2,1)S(1)}, bf16[1,256,768]{2,1,0:T(8,128)(2,1)}, u32[]{:S(2)}) copy-start(bf16[1,256,768]{2,1,0:T(8,128)(2,1)} %param.8) | copy-start | bytes 1179652
  10.9 126.0 %all-gather.7.cloned.1.call-start = ((), (), s32[]{:S(2)}) async-start(), calls=%async_computation.3 | async-start | bytes 1474560 | tf_op jit(solution)/shard_map/all_gather | solution.py:464
  11.7 127.6 %all-gather.9.cloned.1.call-start = ((), (), s32[]{:S(2)}) async-start(), calls=%async_computation.4 | async-start | bytes 4423680 | tf_op jit(solution)/shard_map/all_gather | solution.py:465
  12.4 130.1 %all-gather.11.cloned.1.call-start = ((), (), s32[]{:S(2)}) async-start(), calls=%async_computation.5 | async-start | bytes 2211840 | tf_op jit(solution)/shard_map/all_gather | solution.py:466
  13.0 223.2 %reduce-scatter.3.cloned.1.call-start = ((), (), s32[]{:S(2)}) async-start(), calls=%async_computation.6 | async-start | bytes 8847360 | tf_op jit(solution)/shard_map/reduce_scatter | solution.py:523
  13.2 43.7 %copy-start.21 = (f32[256]{0:T(256)}, f32[256]{0:T(256)S(1)}, u32[]{:S(2)}) copy-start(f32[256]{0:T(256)S(1)} %broadcast_multiply_fusion.1) | copy-start | bytes 3076
  13.5 36.3 %copy-start.25 = (f32[256]{0:T(256)}, f32[256]{0:T(256)S(1)}, u32[]{:S(2)}) copy-start(f32[256]{0:T(256)S(1)} %fusion.20) | copy-start | bytes 3076
  13.5 43.4 %copy-start.23 = (f32[256]{0:T(256)}, f32[256]{0:T(256)S(1)}, u32[]{:S(2)}) copy-start(f32[256]{0:T(256)S(1)} %fusion.39) | copy-start | bytes 3076
  13.7 47.2 %copy-start.15 = (f32[256,32]{0,1:T(8,128)}, f32[256,32]{0,1:T(8,128)S(1)}, u32[]{:S(2)}) copy-start(f32[256,32]{0,1:T(8,128)S(1)} %get-tuple-element.67) | copy-start | bytes 98308
  13.7 47.2 %copy-start.17 = (f32[256,32]{0,1:T(8,128)}, f32[256,32]{0,1:T(8,128)S(1)}, u32[]{:S(2)}) copy-start(f32[256,32]{0,1:T(8,128)S(1)} %get-tuple-element.68) | copy-start | bytes 98308
  139.1 11.2 %copy-start = (f32[256,768]{1,0:T(8,128)}, f32[256,768]{1,0:T(8,128)S(1)}, u32[]{:S(2)}) copy-start(f32[256,768]{1,0:T(8,128)S(1)} %get-tuple-element.70) | copy-start | bytes 2359300
  139.3 3.2 copy-start.11
  145.9 3.1 copy-start.10
  150.3 1.5 copy-start.5
  150.6 2.7 copy-start.6
  151.5 1.7 copy-start.8
  155.7 3.9 %copy-start.2 = (bf16[768,2304]{1,0:T(8,128)(2,1)S(1)}, bf16[768,2304]{1,0:T(8,128)(2,1)}, u32[]{:S(2)}) copy-start(bf16[768,2304]{1,0:T(8,128)(2,1)} %convolution_convert_fusion.1) | copy-start | bytes 10616836
  168.1 155.6 %reduce-scatter.5.cloned.1.call-start = ((), (), s32[]{:S(2)}) async-start(), calls=%async_computation.7 | async-start | bytes 4915200 | tf_op jit(solution)/shard_map/reduce_scatter | solution.py:546
  236.1 2.0 copy-start.14
  240.3 2.1 copy-start.9
  315.8 4.5 %copy-start.7 = (f32[256,768]{1,0:T(8,128)S(1)}, f32[256,768]{1,0:T(8,128)}, u32[]{:S(2)}) copy-start(f32[256,768]{1,0:T(8,128)} %copy-done.6) | copy-start | bytes 2359300
  315.8 4.5 %copy-start.12 = (bf16[1,256,768]{2,1,0:T(8,128)(2,1)S(1)}, bf16[1,256,768]{2,1,0:T(8,128)(2,1)}, u32[]{:S(2)}) copy-start(bf16[1,256,768]{2,1,0:T(8,128)(2,1)} %param.9) | copy-start | bytes 1179652
  315.8 4.5 %copy-start.28 = (f32[256]{0:T(256)S(1)}, f32[256]{0:T(256)}, u32[]{:S(2)}) copy-start(f32[256]{0:T(256)} %copy-done.27) | copy-start | bytes 3076
  (11 other events, 10.6 us)
Sparse Core Ops, SparseCore 0:
  11.1 34.5 all-gather.4
  47.2 17.4 all-gather.6
  66.3 30.8 all-gather.8
  98.6 20.6 all-gather.10
  168.2 63.0 reduce-scatter.2
  246.4 40.8 reduce-scatter.4
